TPU v7x, 256 devices: a whole 4x4x8 slice. The times are simulated.
256 devices in a mesh: space: 32 (over y, z), tm: 8 (over x, core).
Axes of the slice: x: 4, y: 4, z: 8, core: 2. Of those that a mesh axis runs over, the one named last changes fastest.
Arguments:
- snapshots: float32 [4096, 98304], P('tm', 'space')
- sample_phase: int32 [4, 8], replicated, may hold values from 0 to 15, as said below
Outputs:
- residual: float32 [4096, 98304], P('tm', 'space')
Inputs may be any that keep to these rules, and one draw needn't show every extreme that they name: sample_phase[l, w] lies below 4096 / (256 2^l); entries with w >= 2^l are never read.
All inputs are finite; a program needn't handle non-finite values.
Results may differ from a plain program's by a relative error of at most 0.0001.
Values sent between devices are 32-bit elements; how exact they have to be, the bound alone decides.
A program may use at most 64 MiB of HBM per device.

v0:
```python
from functools import partial
import math

import jax
import jax.numpy as jnp
from jax import lax
from jax.sharding import PartitionSpec as P

SNAPS = 4096
NSUB = 256
RANK = 32
LEVELS = 4


precise = lax.Precision.HIGHEST


def cosine_table(position):
    frequency = jnp.arange(RANK, dtype=jnp.float32)
    weights = jnp.where(frequency == 0.0, math.sqrt(1.0 / NSUB), math.sqrt(2.0 / NSUB)).astype(
        jnp.float32
    )
    return (
        jnp.cos(math.pi * (position[:, None] + 0.5) * frequency[None, :] / NSUB) * weights[None, :]
    )


def amplitudes(reduced, window_phase, stride, first_row, count_rows):
    sampled_basis = cosine_table(jnp.arange(NSUB, dtype=jnp.float32))
    earlier = reduced[:, :-1]
    following = reduced[:, 1:]
    identity = jnp.eye(RANK, dtype=jnp.float32)
    lag_gram = jnp.dot(earlier, earlier.T, precision=precise)
    cross_gram = jnp.dot(following, earlier.T, precision=precise)
    ridge_one = 0.1 * jnp.trace(lag_gram) / RANK
    factor_one = jnp.linalg.cholesky(lag_gram + ridge_one * identity)
    operator = jax.scipy.linalg.cho_solve((factor_one, True), cross_gram.T).T
    predicted = jnp.concatenate(
        [reduced[:, :1], jnp.dot(operator, earlier, precision=precise)], axis=1
    )
    smooth_coef = jnp.dot(predicted, sampled_basis, precision=precise)
    mode_gram = jnp.dot(reduced, sampled_basis, precision=precise)
    mode_gram = 0.5 * (mode_gram + mode_gram.T)
    ridge_two = 0.1 * jnp.trace(mode_gram) / RANK
    factor_two = jnp.linalg.cholesky(mode_gram + ridge_two * identity)
    coefficients = jax.scipy.linalg.cho_solve((factor_two, True), smooth_coef)
    rows_index = first_row + jnp.arange(count_rows, dtype=jnp.int32)
    position = (rows_index - window_phase).astype(jnp.float32) / stride
    return jnp.dot(coefficients, cosine_table(position).T, precision=precise)


def body(snapshots, sample_phase):
    snap_rows, point_cols = snapshots.shape
    tm_count = lax.axis_size("tm")
    tm_index = lax.axis_index("tm")
    residual = snapshots
    for tier_index in range(LEVELS):
        width_rows = SNAPS // 2**tier_index
        stride = width_rows // NSUB
        group_size = width_rows // snap_rows
        local_wins = 1
        span_rows = snap_rows // local_wins
        sub_rows = span_rows // stride
        first_window = tm_index // group_size * local_wins
        row_offset = tm_index % group_size * snap_rows
        phases = lax.dynamic_slice_in_dim(sample_phase[tier_index], first_window, local_wins)
        blocks = residual.reshape(local_wins, sub_rows, stride, point_cols)
        selector = (jnp.arange(stride, dtype=jnp.int32)[None, :] == phases[:, None]).astype(
            jnp.float32
        )
        sampled = jnp.einsum("jrsp,js->jrp", blocks, selector, precision=precise)
        position = (row_offset // stride + jnp.arange(sub_rows, dtype=jnp.int32)).astype(
            jnp.float32
        )
        own_basis = cosine_table(position)
        coords = jnp.einsum("rk,jrp->jkp", own_basis, sampled, precision=precise)
        if group_size > 1:
            slot_count = tm_count // group_size
            slot_buffer = jnp.zeros((slot_count, RANK, point_cols), jnp.float32)
            slot_buffer = lax.dynamic_update_slice(
                slot_buffer, coords, (tm_index // group_size, 0, 0)
            )
            summed = lax.psum(slot_buffer, "tm")
            coords = lax.dynamic_slice(
                summed, (tm_index // group_size, 0, 0), (1, RANK, point_cols)
            )
        local_terms = jnp.einsum("jkp,jrp->jkr", coords, sampled, precision=precise)
        window_buffer = jnp.zeros((2**tier_index, RANK, NSUB), jnp.float32)
        window_buffer = lax.dynamic_update_slice(
            window_buffer, local_terms, (first_window, 0, row_offset // stride)
        )
        totals = lax.psum(window_buffer, ("space", "tm"))
        reduced = lax.dynamic_slice(totals, (first_window, 0, 0), (local_wins, RANK, NSUB))
        window_fit = partial(amplitudes, stride=stride, first_row=row_offset, count_rows=span_rows)
        amplitude = jax.vmap(window_fit)(reduced, phases)
        fitted = jnp.einsum("jkc,jkp->jcp", amplitude, coords, precision=precise)
        residual = (residual.reshape(local_wins, span_rows, point_cols) - fitted).reshape(
            snap_rows, point_cols
        )
    return residual


def solution(mesh):
    placed = (P("tm", "space"), P())
    return jax.shard_map(
        body, mesh=mesh, in_specs=placed, out_specs=P("tm", "space"), check_vma=False
    )
```

profile of v0, /device:TPU:1, one launch (start us, length us, event | category | flops | bytes accessed | tf_op | source)
XLA Modules:
  0.0 1231.4 jit_solution(15490973568199184051)
XLA Ops:
  8.0 5.8 fusion.234
  16.6 66.3 %all-reduce.7.cloned.1.call-done = f32[32,3072]{1,0:T(8,128)} async-done(((f32[32,3072]{1,0:T(8,128)}), f32[32,3072]{1,0:T(8,128)}) %all-reduce.7.cloned.1.call-update) | async-done | bytes 393232 | tf_op jit(solution)/shard_map/psum | solution.py:83
  84.9 78.7 %psum.50 = f32[1,32,256]{2,1,0:T(8,128)S(1)} all-reduce(f32[1,32,256]{2,1,0:T(8,128)S(1)} %dynamic_update_slice.21), channel_id=1, replica_groups=mesh['space'=32,'tm'=8] {'space','tm'}, use_global_device_ids=true, to_apply=%region_1.2 | all-reduce | flops 8192 | bytes 65536 | tf_op jit(solution)/shard_map/psum | solution.py:92
  166.7 2.9 custom-call.22
  171.0 2.4 custom-call.25
  174.2 2.9 custom-call.23
  183.9 7.5 convolution_subtract_fusion.3
  191.4 2.7 copy-done
  194.1 3.7 fusion
  200.3 60.7 %all-reduce.9.cloned.1.call-done = f32[2,32,3072]{2,1,0:T(8,128)} async-done(((f32[2,32,3072]{2,1,0:T(8,128)}), f32[2,32,3072]{2,1,0:T(8,128)}) %all-reduce.9.cloned.1.call-update) | async-done | bytes 786448 | tf_op jit(solution)/shard_map/psum | solution.py:83
  265.0 244.6 %all-reduce.11.cloned.1.call-done = f32[2,32,256]{2,1,0:T(8,128)} async-done(((f32[2,32,256]{2,1,0:T(8,128)}), f32[2,32,256]{2,1,0:T(8,128)}) %all-reduce.11.cloned.1.call-update) | async-done | bytes 65552 | tf_op jit(solution)/shard_map/psum | solution.py:92
  512.6 2.9 custom-call.26
  521.7 2.9 custom-call.27
  525.9 2.4 custom-call.28
  533.9 9.0 convolution_subtract_fusion.2
  542.9 7.6 reshape.710
  550.5 9.0 fusion.231
  563.7 62.1 %all-reduce.13.cloned.1.call-done = f32[4,32,3072]{2,1,0:T(8,128)} async-done(((f32[4,32,3072]{2,1,0:T(8,128)}), f32[4,32,3072]{2,1,0:T(8,128)}) %all-reduce.13.cloned.1.call-update) | async-done | bytes 1572880 | tf_op jit(solution)/shard_map/psum | solution.py:83
  625.8 2.6 fusion.21
  629.5 247.8 %all-reduce.15.cloned.1.call-done = f32[4,32,256]{2,1,0:T(8,128)} async-done(((f32[4,32,256]{2,1,0:T(8,128)}), f32[4,32,256]{2,1,0:T(8,128)}) %all-reduce.15.cloned.1.call-update) | async-done | bytes 131088 | tf_op jit(solution)/shard_map/psum | solution.py:92
  880.2 2.9 custom-call.30
  884.5 2.4 custom-call.33
  889.3 2.9 custom-call.31
  901.6 9.0 convolution_subtract_fusion.1
  910.5 8.1 reshape.718
  918.7 15.5 %fusion.239 = f32[1,256,3072]{2,0,1:T(1,128)S(1)} fusion(f32[256,2,3072]{2,1,0:T(2,128)} %reshape.718, s32[]{:T(128)} %bitcast.86), kind=kOutput, calls=%fused_computation.332 | convolution fusion | flops 18874370 | bytes 9437188 | tf_op jit(solution)/shard_map/jrsp,js->jrp/dot_general | solution.py:71
  934.2 2.7 fusion.6
  936.9 2.9 fusion.18
  941.1 250.0 %all-reduce.17.cloned.1.call-done = f32[8,32,256]{2,1,0:T(8,128)} async-done(((f32[8,32,256]{2,1,0:T(8,128)}), f32[8,32,256]{2,1,0:T(8,128)}) %all-reduce.17.cloned.1.call-update) | async-done | bytes 262160 | tf_op jit(solution)/shard_map/psum | solution.py:92
  1194.0 2.9 custom-call.34
  1203.2 2.9 custom-call.35
  1215.5 8.9 convolution_subtract_fusion
  (156 shorter events, 76.0 us)
Async XLA Ops:
  6.5 76.4 %all-reduce.7.cloned.1.call-start = ((), (), s32[]{:S(2)}) async-start(), calls=%async_computation | async-start | bytes 786432 | tf_op jit(solution)/shard_map/psum | solution.py:83
  15.3 245.8 %all-reduce.9.cloned.1.call-start = ((), (), s32[]{:S(2)}) async-start(), calls=%async_computation.1 | async-start | bytes 1572864 | tf_op jit(solution)/shard_map/psum | solution.py:83
  191.4 2.7 copy-start
  198.7 0.9 copy-start.2
  199.6 310.0 %all-reduce.11.cloned.1.call-start = ((), (), s32[]{:S(2)}) async-start(), calls=%async_computation.2 | async-start | bytes 131072 | tf_op jit(solution)/shard_map/psum | solution.py:92
  263.3 0.6 copy-start.5
  263.9 361.9 %all-reduce.13.cloned.1.call-start = ((), (), s32[]{:S(2)}) async-start(), calls=%async_computation.3 | async-start | bytes 3145728 | tf_op jit(solution)/shard_map/psum | solution.py:83
  561.1 1.1 copy-start.1
  562.2 315.1 %all-reduce.15.cloned.1.call-start = ((), (), s32[]{:S(2)}) async-start(), calls=%async_computation.4 | async-start | bytes 262144 | tf_op jit(solution)/shard_map/psum | solution.py:92
  628.7 0.7 copy-start.4
  629.4 561.7 %all-reduce.17.cloned.1.call-start = ((), (), s32[]{:S(2)}) async-start(), calls=%async_computation.5 | async-start | bytes 524288 | tf_op jit(solution)/shard_map/psum | solution.py:92
  939.8 0.7 copy-start.3
Sparse Core Ops, SparseCore 0:
  15.4 67.4 all-reduce.6
  199.7 61.2 all-reduce.8
  266.6 243.0 all-reduce.10
  562.4 63.4 all-reduce.12
  631.2 246.0 all-reduce.14
  940.6 250.4 all-reduce.16
where the time goes:
time: 1240 us; the launch traced here: 1230 us
  waiting for transfers between devices  932 us (75%)
  matrix products  112 us (9%)
  blocking collectives  78.7 us (6%)
  other arithmetic  58.9 us (5%)
  local copies, waits for them, and re-layouts  30.2 us (2%)
  between operations  19.6 us (2%)
    psum x3, waiting for transfers between devices, body(): totals = lax.psum(window_buffer, ('space', 'tm'))  742 us
    psum x3, waiting for transfers between devices, body(): summed = lax.psum(slot_buffer, 'tm')  189 us
    psum x1, blocking collectives, body(): totals = lax.psum(window_buffer, ('space', 'tm'))  78.7 us
    dot_general x4, matrix products, body(): fitted = jnp.einsum('jkc,jkp->jcp', amplitude, coords, precision=precise)  34.3 us
    dot_general x4, matrix products, body(): sampled = jnp.einsum('jrsp,js->jrp', blocks, selector, precision=precise)  34 us
  transfers between devices with their start and end apart: 6, of which 6 were waited for; matrix products, arithmetic and copies ran while one was open for 0% of the time, Pallas kernels for 0%

commit v1 on v0

v1 whole, which is shorter than its diff:
```python
import functools
import math

import jax
import jax.numpy as jnp
import numpy as np
from jax import lax
from jax.experimental import pallas as pl
from jax.experimental.pallas import tpu as pltpu
from jax.sharding import PartitionSpec as P

NSUB = 256
RANK = 32
LEVELS = 4
PATH = RANK * LEVELS
ROWS = 512
COLS = 3072
HALF = COLS // 2
PIECE = HALF // 4
CHUNKS = 32
PACKET = 24
MESH = pl.DeviceIdType.MESH
f32 = jnp.float32
bf16 = jnp.bfloat16
VLIM = 60 * 1024 * 1024


def make_constants():
    j = np.arange(RANK)
    cj = np.where(j == 0, math.sqrt(1.0 / NSUB), math.sqrt(2.0 / NSUB))
    r = np.arange(ROWS)[:, None]
    cos_rows, sin_rows = [], []
    for m in range(LEVELS):
        s = 16 >> m
        ang = math.pi * j * (r + s / 2.0) / (256.0 * s)
        cos_rows.append(cj * np.cos(ang))
        sin_rows.append(cj * np.sin(ang))
    cos_rows = np.concatenate(cos_rows, 1).astype(np.float32)
    sin_rows = np.concatenate(sin_rows, 1).astype(np.float32)
    k = np.arange(NSUB)[:, None]
    bc = np.zeros((3, NSUB, PATH))
    bs = np.zeros((3, NSUB, PATH))
    for l in range(1, LEVELS):
        for m in range(l):
            ang = math.pi * j * (k * 2.0 ** (m - l) + 0.5) / 256.0
            bc[l - 1, :, m * RANK : (m + 1) * RANK] = cj * np.cos(ang)
            bs[l - 1, :, m * RANK : (m + 1) * RANK] = cj * np.sin(ang)
    q = cj * np.cos(math.pi * j * (k + 0.5) / 256.0)
    qpad = np.zeros((NSUB, PATH))
    qpad[:, :RANK] = q
    wq = np.zeros((NSUB, PATH))
    wq[: NSUB - 1, 64:96] = q[1:]
    wq[:, 96:128] = q
    first = np.zeros((NSUB, PATH))
    first[0, 64:96] = q[0]
    small = np.stack([qpad, wq, first]).astype(np.float32)
    return cos_rows, sin_rows, bc.astype(np.float32), bs.astype(np.float32), small


def cos_sin(num, period):
    frac = num.astype(f32) * (1.0 / period.astype(f32))
    quarter = jnp.floor(frac * 4.0 + 0.5)
    a = (frac - quarter * 0.25) * (2.0 * math.pi)
    a2 = a * a
    c = 1.0 + a2 * (-0.5 + a2 * (1 / 24.0 + a2 * (-1 / 720.0 + a2 * (1 / 40320.0))))
    s = a * (1.0 + a2 * (-1 / 6.0 + a2 * (1 / 120.0 + a2 * (-1 / 5040.0 + a2 * (1 / 362880.0)))))
    qi = quarter.astype(jnp.int32) & 3
    cosv = jnp.where(qi == 0, c, jnp.where(qi == 1, -s, jnp.where(qi == 2, -c, s)))
    sinv = jnp.where(qi == 0, s, jnp.where(qi == 1, c, jnp.where(qi == 2, -s, -c)))
    return cosv, sinv


def path_phases(phase_ref, t):
    return [phase_ref[m, t // (8 >> m)] for m in range(LEVELS)]


def pick(level, values):
    out = jnp.where(level == 0, values[0], values[1])
    out = jnp.where(level == 2, values[2], out)
    return jnp.where(level == 3, values[3], out)


def lane_turn(idx, offsets):
    level, j = idx // RANK, idx % RANK
    period = pick(level, [512 * 16, 512 * 8, 512 * 4, 512 * 2])
    num = (j * pick(level, offsets)) & (period - 1)
    return cos_sin(num, period)


def split(x):
    hi = x.astype(bf16)
    lo = (x - hi.astype(f32)).astype(bf16)
    return hi, lo


def dot(a, b, dims):
    return lax.dot_general(a, b, (dims, ((), ())), preferred_element_type=f32)


def dot32(a, b, ca, cb):
    return lax.dot_general(
        a, b, (((ca,), (cb,)), ((), ())), precision=lax.Precision.HIGHEST, preferred_element_type=f32
    )


def project_kernel(phase_ref, cos_ref, sin_ref, x_ref, p_ref, d_ref):
    @pl.when(pl.program_id(0) == 0)
    def _():
        t = lax.axis_index("tm")
        ps = path_phases(phase_ref, t)
        idx = lax.broadcasted_iota(jnp.int32, (PATH, 1), 0)
        offsets = [(t % (8 >> m)) * ROWS - ps[m] for m in range(LEVELS)]
        c, s = lane_turn(idx, offsets)
        level = idx // RANK
        r = lax.broadcasted_iota(jnp.int32, (PATH, ROWS), 1)
        stride = pick(level, [16, 8, 4, 2])
        on = ((r - pick(level, ps)) & (stride - 1)) == 0
        d = jnp.where(on, cos_ref[...] * c - sin_ref[...] * s, 0.0)
        hi, lo = split(d)
        d_ref[:PATH, :] = hi
        d_ref[PATH:, :] = lo

    xh, xl = split(x_ref[...])
    d = d_ref[...]
    a = dot(d, xh, ((1,), (0,)))
    b = dot(d[:PATH], xl, ((1,), (0,)))
    p_ref[...] = a[:PATH] + (a[PATH:] + b)


def project(phase, cos_t, sin_t, x):
    tile = 512
    return pl.pallas_call(
        project_kernel,
        grid=(COLS // tile,),
        in_specs=[
            pl.BlockSpec(memory_space=pltpu.SMEM),
            pl.BlockSpec((PATH, ROWS), lambda i: (0, 0)),
            pl.BlockSpec((PATH, ROWS), lambda i: (0, 0)),
            pl.BlockSpec((ROWS, tile), lambda i: (0, i)),
        ],
        out_specs=pl.BlockSpec((PATH, tile), lambda i: (0, i)),
        out_shape=jax.ShapeDtypeStruct((PATH, COLS), f32),
        scratch_shapes=[pltpu.VMEM((2 * PATH, ROWS), bf16)],
        compiler_params=pltpu.CompilerParams(vmem_limit_bytes=VLIM),
        name="project",
    )(phase, cos_t, sin_t, x)


def remote(src, dst, send, recv, where):
    return pltpu.make_async_remote_copy(
        src_ref=src, dst_ref=dst, send_sem=send, recv_sem=recv, device_id=where, device_id_type=MESH
    )


def sum_kernel(p_ref, y_ref, r1, s0, s1, r2, r3, ssem, rsem):
    t = lax.axis_index("tm")
    x, h = t // 2, t % 2
    partner = {"tm": x * 2 + 1 - h}
    across = [{"tm": lax.rem(x + d, 4) * 2 + h} for d in range(1, 4)]
    pair = {"tm": (x + 1 - 2 * (x % 2)) * 2 + h}
    barrier = pltpu.get_barrier_semaphore()
    for dev in [partner] + across:
        pl.semaphore_signal(barrier, inc=1, device_id=dev, device_id_type=MESH)
    pl.semaphore_wait(barrier, 4)

    mine = pl.multiple_of(h * HALF, 128)
    other = pl.multiple_of((1 - h) * HALF, 128)
    own = pl.ds(mine, HALF)
    live = []

    def go(i, src, dst, where):
        c = remote(src, dst, ssem.at[i], rsem.at[i], where)
        c.start()
        live.append(c)
        return c

    first = [
        go(l, p_ref.at[pl.ds(32 * l, 32), pl.ds(other, HALF)], r1.at[l], partner) for l in range(3)
    ]
    y_ref[96:128, :] = p_ref[96:128, :]
    first[0].wait_recv()
    s0[...] = p_ref[0:32, own] + r1[0]
    spread = []
    for d in range(1, 4):
        col = pl.multiple_of(lax.rem(x + d, 4) * PIECE, 128)
        spread.append(go(2 + d, s0.at[:, pl.ds(col, PIECE)], r3.at[d - 1], across[d - 1]))
    first[1].wait_recv()
    s1[...] = p_ref[32:64, own] + r1[1]
    swap = go(6, s1, r2, pair)
    first[2].wait_recv()
    y_ref[64:96, own] = p_ref[64:96, own] + r1[2]
    last2 = go(7, y_ref.at[64:96, own], y_ref.at[64:96, own], partner)
    for c in spread:
        c.wait_recv()
    spot = pl.ds(pl.multiple_of(mine + x * PIECE, 128), PIECE)
    y_ref[0:32, spot] = (s0[:, pl.ds(pl.multiple_of(x * PIECE, 128), PIECE)] + r3[0]) + (r3[1] + r3[2])
    place = y_ref.at[0:32, spot]
    back = [go(8 + d, place, place, across[d - 1]) for d in range(1, 4)]
    pass_on = [go(12, place, place, partner)]
    swap.wait_recv()
    y_ref[32:64, own] = s1[...] + r2[...]
    last1 = go(13, y_ref.at[32:64, own], y_ref.at[32:64, own], partner)
    for d in range(1, 4):
        back[d - 1].wait_recv()
        got = pl.ds(pl.multiple_of(mine + lax.rem(x + 4 - d, 4) * PIECE, 128), PIECE)
        pass_on.append(go(13 + d, y_ref.at[0:32, got], y_ref.at[0:32, got], partner))
    for c in pass_on + [last1, last2]:
        c.wait_recv()
    for c in live:
        c.wait_send()


def sum_over_time(p):
    return pl.pallas_call(
        sum_kernel,
        in_specs=[pl.BlockSpec(memory_space=pltpu.VMEM)],
        out_specs=pl.BlockSpec(memory_space=pltpu.VMEM),
        out_shape=jax.ShapeDtypeStruct((PATH, COLS), f32),
        scratch_shapes=[
            pltpu.VMEM((3, RANK, HALF), f32),
            pltpu.VMEM((RANK, HALF), f32),
            pltpu.VMEM((RANK, HALF), f32),
            pltpu.VMEM((RANK, HALF), f32),
            pltpu.VMEM((3, RANK, PIECE), f32),
            pltpu.SemaphoreType.DMA((17,)),
            pltpu.SemaphoreType.DMA((17,)),
        ],
        compiler_params=pltpu.CompilerParams(
            collective_id=0, has_side_effects=True, vmem_limit_bytes=VLIM
        ),
        name="sum_over_time",
    )(p)


def product_kernel(phase_ref, x_ref, y_ref, f_ref, acc):
    i = pl.program_id(0)
    xh, xl = split(x_ref[...])
    yh, yl = split(y_ref[...])
    both = jnp.concatenate([yh, yl], axis=0)
    a = dot(xh, both, ((1,), (1,)))
    b = dot(xl, yh, ((1,), (1,)))
    new = a[:, :PATH] + (a[:, PATH:] + b)

    @pl.when(i == 0)
    def _():
        acc[...] = new

    @pl.when(i > 0)
    def _():
        acc[...] += new

    @pl.when(i == pl.num_programs(0) - 1)
    def _():
        t = lax.axis_index("tm")
        ps = path_phases(phase_ref, t)
        row = 0
        for l in (3, 2, 1, 0):
            for e in range(1 << l):
                start = ps[l] + e * (16 >> l)
                f_ref[pl.ds(row, CHUNKS, stride=16), :] = acc[pl.ds(start, CHUNKS, stride=16), :]
                row += 1
        f_ref[pl.ds(row, CHUNKS, stride=16), :] = jnp.zeros((CHUNKS, PATH), f32)


def products(phase, x, y):
    tile = 512
    return pl.pallas_call(
        product_kernel,
        grid=(COLS // tile,),
        in_specs=[
            pl.BlockSpec(memory_space=pltpu.SMEM),
            pl.BlockSpec((ROWS, tile), lambda i: (0, i)),
            pl.BlockSpec((PATH, tile), lambda i: (0, i)),
        ],
        out_specs=pl.BlockSpec((ROWS, PATH), lambda i: (0, 0)),
        out_shape=jax.ShapeDtypeStruct((ROWS, PATH), f32),
        scratch_shapes=[pltpu.VMEM((ROWS, PATH), f32)],
        compiler_params=pltpu.CompilerParams(vmem_limit_bytes=VLIM),
        name="products",
    )(phase, x, y)


def gather_kernel(f_ref, g_ref, ry, q, rz, xb, cb, ssem, rsem):
    s = lax.axis_index("space")
    t = lax.axis_index("tm")
    y, z = s // 8, s % 8
    ys = [lax.rem(y + d, 4) for d in range(1, 4)]
    zs = [lax.rem(z + d, 8) for d in range(1, 8)]
    ts = [lax.rem(t + d, 8) for d in range(1, 8)]
    to_y = [{"space": v * 8 + z} for v in ys]
    to_z = [{"space": y * 8 + v} for v in zs]
    to_t = [{"tm": v} for v in ts]
    barrier = pltpu.get_barrier_semaphore()
    for dev in to_y + to_z + to_t:
        pl.semaphore_signal(barrier, inc=1, device_id=dev, device_id_type=MESH)
    pl.semaphore_wait(barrier, 17)
    live = []

    def go(i, src, dst, where):
        c = remote(src, dst, ssem.at[i], rsem.at[i], where)
        c.start()
        live.append(c)
        return c

    def rows(start, n):
        return pl.ds(pl.multiple_of(start, 8), n)

    a = [go(d, f_ref.at[rows(ys[d] * 128, 128)], ry.at[d], to_y[d]) for d in range(3)]
    for c in a:
        c.wait_recv()
    q[...] = (f_ref[rows(y * 128, 128), :] + ry[0]) + (ry[1] + ry[2])
    a = [go(3 + d, q.at[rows(zs[d] * 16, 16)], rz.at[d], to_z[d]) for d in range(7)]
    for c in a:
        c.wait_recv()
    ch = q[rows(z * 16, 16), :] + rz[0]
    for d in range(1, 7):
        ch = ch + rz[d]
    base = s * PACKET
    g_ref[rows(base, 8), :] = ch[0:8]
    xb[t] = ch[8:16]
    a = [go(10 + d, xb.at[t], xb.at[t], to_t[d]) for d in range(7)]
    for c in a:
        c.wait_recv()
    pair = t // 2 * 2
    quad = t // 4 * 4
    g_ref[rows(base + 8, 8), :] = jnp.concatenate([xb[pair][0:4], xb[pair + 1][0:4]], axis=0)
    for i in range(4):
        cb[2 * i : 2 * i + 2, :] = xb[quad + i][4:6]
    for i in range(8):
        cb[8 + i : 9 + i, :] = xb[i][6:7]
    lane = lax.broadcasted_iota(jnp.int32, (8, PATH), 1)
    g_ref[rows(base + 16, 8), :] = jnp.where(lane < 64, cb[0:8, :], pltpu.roll(cb[8:16, :], 64, 1))
    piece = g_ref.at[rows(base, PACKET)]
    a = [go(17 + d, piece, piece, to_z[d]) for d in range(7)]
    for c in a:
        c.wait_recv()
    band = g_ref.at[rows(y * 8 * PACKET, 8 * PACKET)]
    a = [go(24 + d, band, band, to_y[d]) for d in range(3)]
    for c in a:
        c.wait_recv()
    for c in live:
        c.wait_send()


def gather(f):
    return pl.pallas_call(
        gather_kernel,
        in_specs=[pl.BlockSpec(memory_space=pltpu.VMEM)],
        out_specs=pl.BlockSpec(memory_space=pltpu.VMEM),
        out_shape=jax.ShapeDtypeStruct((CHUNKS * PACKET, PATH), f32),
        scratch_shapes=[
            pltpu.VMEM((3, 128, PATH), f32),
            pltpu.VMEM((128, PATH), f32),
            pltpu.VMEM((7, 16, PATH), f32),
            pltpu.VMEM((8, 8, PATH), f32),
            pltpu.VMEM((16, PATH), f32),
            pltpu.SemaphoreType.DMA((27,)),
            pltpu.SemaphoreType.DMA((27,)),
        ],
        compiler_params=pltpu.CompilerParams(
            collective_id=1, has_side_effects=True, vmem_limit_bytes=VLIM
        ),
        name="gather",
    )(f)


def eliminate(a, b):
    sub = lax.broadcasted_iota(jnp.int32, (RANK, 1), 0)
    for k in range(RANK):
        ra = a[k : k + 1, :]
        rb = b[k : k + 1, :]
        ra = ra / a[k : k + 1, k : k + 1]
        rb = rb / b[k : k + 1, k : k + 1]
        a = jnp.where(sub == k, ra, a - a[:, k : k + 1] * ra)
        b = jnp.where(sub == k, rb, b - b[:, k : k + 1] * rb)
    return a, b


def solve_kernel(phase_ref, bc_ref, bs_ref, small_ref, g_ref, n_ref, lv):
    t = lax.axis_index("tm")
    ps = path_phases(phase_ref, t)
    lane = lax.broadcasted_iota(jnp.int32, (1, PATH), 1)
    row = lax.broadcasted_iota(jnp.int32, (NSUB, 1), 0)
    big = CHUNKS * PACKET
    for c in range(CHUNKS):
        lv[3, 8 * c : 8 * c + 8, :] = g_ref[PACKET * c : PACKET * c + 8, :]
    for i in range(2):
        for e in range(4):
            lv[2, pl.ds(128 * i + e, CHUNKS, stride=4), :] = g_ref[
                pl.ds(8 + 4 * i + e, CHUNKS, stride=PACKET), :
            ]
    for i in range(4):
        for e in range(2):
            lv[1, pl.ds(64 * i + e, CHUNKS, stride=2), :] = g_ref[
                pl.ds(16 + 2 * i + e, CHUNKS, stride=PACKET), :
            ]
    for i in range(8):
        lv[0, 32 * i : 32 * i + 32, :] = pltpu.roll(
            g_ref[pl.ds(16 + i, CHUNKS, stride=PACKET), :], 64, 1
        )
    qpad = small_ref[0]
    wq = small_ref[1]
    first = small_ref[2]
    seen = []
    gram = []
    for l in range(LEVELS):
        m = jnp.where(lane < RANK * (l + 1), lv[l], 0.0)
        seen.append(m)
        gram.append(dot32(qpad, m, 0, 0)[:RANK])
    low = jnp.concatenate(gram, axis=0)
    up = low.T
    rb = lax.broadcasted_iota(jnp.int32, (PATH, PATH), 0) // RANK
    cb = lax.broadcasted_iota(jnp.int32, (PATH, PATH), 1) // RANK
    gram = jnp.where(cb <= rb, low, up)
    tables, folded = [None], [None]
    for l in range(1, LEVELS):
        here = (t // (8 >> l)) * (ROWS * (8 >> l)) + ps[l]
        offsets = [here - (t // (8 >> m)) * (ROWS * (8 >> m)) - ps[m] for m in range(LEVELS)]
        c, s = lane_turn(lane, offsets)
        table = bc_ref[l - 1] * c - bs_ref[l - 1] * s
        tables.append(table)
        folded.append(dot32(qpad, table, 0, 0)[:RANK])
    sub = lax.broadcasted_iota(jnp.int32, (RANK, PATH), 0)
    lan = lax.broadcasted_iota(jnp.int32, (RANK, PATH), 1)
    eye = (sub == lan).astype(f32)
    eye_next = (sub + RANK == lan).astype(f32)
    n = jnp.zeros((PATH, PATH), f32)
    nk = jnp.zeros((PATH, PATH), f32)
    for l in range(LEVELS):
        comb = (sub + RANK * l == lan).astype(f32)
        part = seen[l]
        if l:
            comb = comb - dot32(folded[l], n, 1, 0)
            part = part - dot32(tables[l], nk, 1, 0)
        wide = jnp.concatenate([comb, jnp.zeros((PATH - RANK, PATH), f32)], axis=0)
        rt = dot32(part, wide, 1, 1)
        right = (
            jnp.where(row < NSUB - 1, rt, 0.0)
            + pltpu.roll(jnp.where(row > 0, pltpu.roll(rt, RANK, 1), 0.0), NSUB - 1, 0)
            + wq
        )
        narrow = rt[:, :RANK]
        w = dot32(narrow, right, 0, 0)
        head = dot32(narrow, first, 0, 0)
        wt = dot32(qpad[:, :RANK], rt, 0, 0)
        ridge_one = 0.1 / RANK * jnp.sum(w * eye)
        mode = jnp.where(lan < RANK, 0.5 * (pltpu.roll(w, RANK, 1) + wt), 0.0)
        ridge_two = 0.1 / RANK * jnp.sum(mode * eye)
        a, b = eliminate(w + ridge_one * eye, mode + ridge_two * eye + eye_next)
        smooth = head + dot32(w, a, 0, 0)[RANK : 2 * RANK]
        coef = dot32(b, smooth, 0, 0)[RANK : 2 * RANK]
        new = dot32(coef, comb, 0, 0)[64:96]
        n_ref[RANK * l : RANK * (l + 1), :] = new
        if l < LEVELS - 1:
            before = [n[: RANK * l]] if l else []
            after = [jnp.zeros((PATH - RANK * (l + 1), PATH), f32)]
            n = jnp.concatenate(before + [new] + after, axis=0)
            before = [nk[: RANK * l]] if l else []
            nk = jnp.concatenate(before + [dot32(new, gram, 1, 0)] + after, axis=0)


def solve(phase, bc, bs, small, g):
    vm = pl.BlockSpec(memory_space=pltpu.VMEM)
    return pl.pallas_call(
        solve_kernel,
        in_specs=[pl.BlockSpec(memory_space=pltpu.SMEM), vm, vm, vm, vm],
        out_specs=vm,
        out_shape=jax.ShapeDtypeStruct((PATH, PATH), f32),
        scratch_shapes=[pltpu.VMEM((LEVELS, NSUB, PATH), f32)],
        compiler_params=pltpu.CompilerParams(vmem_limit_bytes=VLIM),
        name="solve",
    )(phase, bc, bs, small, g)


def subtract_kernel(phase_ref, cos_ref, sin_ref, n_ref, x_ref, y_ref, o_ref, e_ref):
    @pl.when(pl.program_id(0) == 0)
    def _():
        t = lax.axis_index("tm")
        ps = path_phases(phase_ref, t)
        idx = lax.broadcasted_iota(jnp.int32, (1, PATH), 1)
        offsets = [(t % (8 >> m)) * ROWS - ps[m] for m in range(LEVELS)]
        c, s = lane_turn(idx, offsets)
        table = cos_ref[...] * c - sin_ref[...] * s
        e = dot32(table, n_ref[...], 1, 0)
        hi, lo = split(e)
        e_ref[:, :PATH] = hi
        e_ref[:, PATH:] = lo

    yh, yl = split(y_ref[...])
    e = e_ref[...]
    fit = dot(e, jnp.concatenate([yh, yh], axis=0), ((1,), (0,)))
    fit = fit + dot(e[:, :PATH], yl, ((1,), (0,)))
    o_ref[...] = x_ref[...] - fit


def subtract(phase, cos_r, sin_r, n, x, y):
    tile = 512
    return pl.pallas_call(
        subtract_kernel,
        grid=(COLS // tile,),
        in_specs=[
            pl.BlockSpec(memory_space=pltpu.SMEM),
            pl.BlockSpec((ROWS, PATH), lambda i: (0, 0)),
            pl.BlockSpec((ROWS, PATH), lambda i: (0, 0)),
            pl.BlockSpec((PATH, PATH), lambda i: (0, 0)),
            pl.BlockSpec((ROWS, tile), lambda i: (0, i)),
            pl.BlockSpec((PATH, tile), lambda i: (0, i)),
        ],
        out_specs=pl.BlockSpec((ROWS, tile), lambda i: (0, i)),
        out_shape=jax.ShapeDtypeStruct((ROWS, COLS), f32),
        scratch_shapes=[pltpu.VMEM((ROWS, 2 * PATH), bf16)],
        compiler_params=pltpu.CompilerParams(vmem_limit_bytes=VLIM),
        name="subtract",
    )(phase, cos_r, sin_r, n, x, y)


def body(snapshots, sample_phase):
    cos_r, sin_r, bc, bs, small = make_constants()
    p = project(sample_phase, jnp.asarray(cos_r.T.copy()), jnp.asarray(sin_r.T.copy()), snapshots)
    y = sum_over_time(p)
    f = products(sample_phase, snapshots, y)
    g = gather(f)
    n = solve(sample_phase, jnp.asarray(bc), jnp.asarray(bs), jnp.asarray(small), g)
    return subtract(sample_phase, jnp.asarray(cos_r), jnp.asarray(sin_r), n, snapshots, y)


def solution(mesh):
    return jax.shard_map(
        body,
        mesh=mesh,
        in_specs=(P("tm", "space"), P()),
        out_specs=P("tm", "space"),
        check_vma=False,
    )
```

time: 1240 us -> 99.4 us (0.08)
  waiting for transfers between devices: 932 us -> 0 us
  matrix products: 112 us -> 0 us
  Pallas kernels: 0 us -> 98.9 us
  blocking collectives: 78.7 us -> 0 us
  other arithmetic: 58.9 us -> 0 us
  local copies, waits for them, and re-layouts: 30.2 us -> 0 us
  between operations: 19.6 us -> 0.02 us
    psum x6 -> x0, waiting for transfers between devices: 932 us -> none  [the longest x3 742 us: body(): totals = lax.psum(window_buffer, ('space', 'tm'))]
    dot_general x40 -> x0, matrix products: 109 us -> none  [the longest x4 34.3 us: body(): fitted = jnp.einsum('jkc,jkp->jcp', amplitude, coords, precision=precise)]
    pallas_call x0 -> x6, Pallas kernels: none -> 98.9 us  [the longest x1 34.6 us: gather(): pl.pallas_call(gather_kernel, in_specs=[pl.BlockSpec(memory_space=pltpu.V...]
    psum x1 -> x0, blocking collectives: 78.7 us -> none  [body(): totals = lax.psum(window_buffer, ('space', 'tm'))]
    another operation x40 -> x0, other arithmetic: 53.6 us -> none  [the longest x12 14.6 us: amplitudes(): factor_two = jnp.linalg.cholesky(mode_gram + ridge_two * identity)]
    another operation x2 -> x0, local copies, waits for them, and re-layouts: 15.7 us -> none
  transfers between devices with their start and end apart: 6 -> 0, of which waited for: 6 -> 0; matrix products, arithmetic and copies ran while one was open for 0% -> 0% of each run, Pallas kernels for 0% -> 0%
where the time goes in v1:
time: 99.4 us; the launch traced here: 98.9 us
  Pallas kernels  98.9 us (99%)
    pallas_call x1, Pallas kernels, gather(): pl.pallas_call(gather_kernel, in_specs=[pl.BlockSpec(memory_space=pltpu.V...  34.6 us
    pallas_call x1, Pallas kernels, solve(): pl.pallas_call(solve_kernel, in_specs=[pl.BlockSpec(memory_space=pltpu.SM...  21.9 us
    pallas_call x1, Pallas kernels, sum_over_time(): pl.pallas_call(sum_kernel, in_specs=[pl.BlockSpec(memory_space=pltpu.VMEM...  19.9 us
    pallas_call x1, Pallas kernels, subtract(): pl.pallas_call(subtract_kernel, grid=(COLS // tile,), in_specs=[pl.BlockS...  8.75 us
    pallas_call x1, Pallas kernels, products(): pl.pallas_call(product_kernel, grid=(COLS // tile,), in_specs=[pl.BlockSp...  6.93 us
    pallas_call x1, Pallas kernels, project(): pl.pallas_call(project_kernel, grid=(COLS // tile,), in_specs=[pl.BlockSp...  6.82 us

profile of v1, /device:TPU:1, one launch (start us, length us, event | category | flops | bytes accessed | tf_op | source)
XLA Modules:
  0.0 98.9 jit_solution(8428348698632744197)
XLA Ops:
  0.0 6.8 %project.1.p_ref = f32[128,3072]{1,0:T(8,128)} custom-call(s32[4,8]{1,0:T(4,128)} %phase_ref.7, f32[128,512]{1,0:T(8,128)} %constant.14.clone.cos_ref, f32[128,512]{1,0:T(8,128)} %constant.15.clone.sin_ref, f32[512,3072]{1,0:T(8,128)} %x_ref.5), custom_call_target="tpu_custom_call" | custom-call | tf_op jit(solution)/shard_map/project/pallas_call | solution.py:132
  6.8 19.9 %sum_over_time.1.y_ref = f32[128,3072]{1,0:T(8,128)} custom-call(f32[128,3072]{1,0:T(8,128)} %project.1.p_ref), custom_call_target="tpu_custom_call" | custom-call | tf_op jit(solution)/shard_map/sum_over_time/pallas_call | solution.py:214
  26.7 6.9 %products.1.f_ref = f32[512,128]{1,0:T(8,128)} custom-call(s32[4,8]{1,0:T(4,128)} %phase_ref.7, f32[512,3072]{1,0:T(8,128)} %x_ref.5, f32[128,3072]{1,0:T(8,128)} %sum_over_time.1.y_ref), custom_call_target="tpu_custom_call" | custom-call | tf_op jit(solution)/shard_map/products/pallas_call | solution.py:267
  33.6 34.6 %gather.1.g_ref = f32[768,128]{1,0:T(8,128)} custom-call(f32[512,128]{1,0:T(8,128)} %products.1.f_ref), custom_call_target="tpu_custom_call" | custom-call | tf_op jit(solution)/shard_map/gather/pallas_call | solution.py:346
  68.3 21.9 %solve.1.n_ref = f32[128,128]{1,0:T(8,128)} custom-call(s32[4,8]{1,0:T(4,128)} %phase_ref.7, f32[3,256,128]{2,1,0:T(8,128)} %constant.16.clone.bc_ref, f32[3,256,128]{2,1,0:T(8,128)} %constant.17.clone.bs_ref, f32[3,256,128]{2,1,0:T(8,128)} %constant.18.clone.small_ref, f32[768,128]{1,0:T(8,128)} %gather.1.g_ref), custom_call_target="tpu_custom_call" | custom-call | tf_op jit(solution)/shard_map/solve/pallas_call | solution.py:464
  90.1 8.7 %subtract.1 = f32[512,3072]{1,0:T(8,128)} custom-call(s32[4,8]{1,0:T(4,128)} %phase_ref.7, f32[512,128]{1,0:T(8,128)} %constant.19.clone.cos_ref, f32[512,128]{1,0:T(8,128)} %constant.20.clone.sin_ref, f32[128,128]{1,0:T(8,128)} %solve.1.n_ref, f32[512,3072]{1,0:T(8,128)} %x_ref.5, f32[128,3072]{1,0:T(8,128)} %sum_over_time.1.y_ref), custom_call_target="tpu_custom_call" | custom-call | tf_op jit(solution)/shard_map/subtract/pallas_call | solution.py:498

commit v2 on v0

v2 whole, which is shorter than its diff:
```python
import functools
import math

import jax
import jax.numpy as jnp
import numpy as np
from jax import lax
from jax.experimental import pallas as pl
from jax.experimental.pallas import tpu as pltpu
from jax.sharding import PartitionSpec as P

NSUB = 256
RANK = 32
LEVELS = 4
PATH = RANK * LEVELS
ROWS = 512
COLS = 3072
HALF = COLS // 2
PIECE = HALF // 4
CHUNKS = 32
STEP = 512
MESH = pl.DeviceIdType.MESH
f32 = jnp.float32
bf16 = jnp.bfloat16
VLIM = 60 * 1024 * 1024


def make_constants():
    j = np.arange(RANK)
    cj = np.where(j == 0, math.sqrt(1.0 / NSUB), math.sqrt(2.0 / NSUB))
    r = np.arange(ROWS)[:, None]
    cos_rows, sin_rows = [], []
    for m in range(LEVELS):
        s = 16 >> m
        ang = math.pi * j * (r + s / 2.0) / (256.0 * s)
        cos_rows.append(cj * np.cos(ang))
        sin_rows.append(cj * np.sin(ang))
    cos_rows = np.concatenate(cos_rows, 1).T.astype(np.float32)
    sin_rows = np.concatenate(sin_rows, 1).T.astype(np.float32)
    k = np.arange(NSUB)[:, None]
    bc = np.zeros((3, NSUB, PATH))
    bs = np.zeros((3, NSUB, PATH))
    for l in range(1, LEVELS):
        for m in range(l):
            ang = math.pi * j * (k * 2.0 ** (m - l) + 0.5) / 256.0
            bc[l - 1, :, m * RANK : (m + 1) * RANK] = cj * np.cos(ang)
            bs[l - 1, :, m * RANK : (m + 1) * RANK] = cj * np.sin(ang)
    q = cj * np.cos(math.pi * j * (k + 0.5) / 256.0)
    qpad = np.zeros((NSUB, PATH))
    qpad[:, :RANK] = q
    wq = np.zeros((NSUB, PATH))
    wq[: NSUB - 1, 64:96] = q[1:]
    wq[:, 96:128] = q
    first = np.zeros((NSUB, PATH))
    first[0, 64:96] = q[0]
    small = np.stack([qpad, wq, first]).astype(np.float32)
    return cos_rows, sin_rows, bc.astype(np.float32), bs.astype(np.float32), small


def cos_sin(num, period):
    frac = num.astype(f32) * (1.0 / period.astype(f32))
    quarter = jnp.floor(frac * 4.0 + 0.5)
    a = (frac - quarter * 0.25) * (2.0 * math.pi)
    a2 = a * a
    c = 1.0 + a2 * (-0.5 + a2 * (1 / 24.0 + a2 * (-1 / 720.0 + a2 * (1 / 40320.0))))
    s = a * (1.0 + a2 * (-1 / 6.0 + a2 * (1 / 120.0 + a2 * (-1 / 5040.0 + a2 * (1 / 362880.0)))))
    qi = quarter.astype(jnp.int32) & 3
    cosv = jnp.where(qi == 0, c, jnp.where(qi == 1, -s, jnp.where(qi == 2, -c, s)))
    sinv = jnp.where(qi == 0, s, jnp.where(qi == 1, c, jnp.where(qi == 2, -s, -c)))
    return cosv, sinv


def path_phases(phase_ref, t):
    return [phase_ref[m, t // (8 >> m)] for m in range(LEVELS)]


def pick(level, values):
    out = jnp.where(level == 0, values[0], values[1])
    out = jnp.where(level == 2, values[2], out)
    return jnp.where(level == 3, values[3], out)


def lane_turn(idx, offsets):
    level, j = idx // RANK, idx % RANK
    period = pick(level, [512 * 16, 512 * 8, 512 * 4, 512 * 2])
    num = (j * pick(level, offsets)) & (period - 1)
    return cos_sin(num, period)


def split(x):
    hi = x.astype(bf16)
    lo = (x - hi.astype(f32)).astype(bf16)
    return hi, lo


def dot(a, b, dims):
    return lax.dot_general(a, b, (dims, ((), ())), preferred_element_type=f32)


def dot32(a, b, ca, cb):
    return lax.dot_general(
        a, b, (((ca,), (cb,)), ((), ())), precision=lax.Precision.HIGHEST, preferred_element_type=f32
    )


def remote(src, dst, send, recv, where):
    return pltpu.make_async_remote_copy(
        src_ref=src, dst_ref=dst, send_sem=send, recv_sem=recv, device_id=where, device_id_type=MESH
    )


def eliminate(a, b):
    block = 8
    sub = lax.broadcasted_iota(jnp.int32, (RANK, 1), 0)
    mats = [a, b]
    for k0 in range(0, RANK, block):
        cols = [
            [jnp.broadcast_to(m[:, k0 + i : k0 + i + 1], (RANK, PATH)) for i in range(block)]
            for m in mats
        ]
        for i in range(block):
            k = k0 + i
            for v in range(2):
                ci = cols[v][i]
                inv = 1.0 / ci[k : k + 1]
                top = mats[v][k : k + 1] * inv
                for j in range(i + 1, block):
                    cj = cols[v][j]
                    sc = cj[k : k + 1] * inv
                    cols[v][j] = jnp.where(sub == k, sc, cj - ci * sc)
                mats[v] = jnp.where(sub == k, top, mats[v] - ci * top)
    return mats[0], mats[1]


def fit_kernel(
    phase_ref, x_hbm, cos_hbm, sin_hbm, bc_hbm, bs_hbm, small_hbm, n_ref, y_hbm,
    xs, ys, p, r1, sb, r2, r3, cs, bcs, bss, small_ref, acc, fa, fb,
    rya, ryb, qa, qb, rza, rzb, xb, cb, gc, gb, gt, lv, tab, fold, xsem, csem, ssem, rsem,
):
    s = lax.axis_index("space")
    t = lax.axis_index("tm")
    yy, zz = s // 8, s % 8
    x, h = t // 2, t % 2
    ps = path_phases(phase_ref, t)
    y_to = [lax.rem(yy + d, 4) for d in range(1, 4)]
    z_to = [lax.rem(zz + d, 8) for d in range(1, 8)]
    dev_y = [{"space": v * 8 + zz} for v in y_to]
    dev_z = [{"space": yy * 8 + v} for v in z_to]
    dev_t = [{"tm": lax.rem(t + d, 8)} for d in range(1, 8)]
    partner = {"tm": x * 2 + 1 - h}
    across = [{"tm": lax.rem(x + d, 4) * 2 + h} for d in range(1, 4)]
    pair_x = {"tm": (x + 1 - 2 * (x % 2)) * 2 + h}

    barrier = pltpu.get_barrier_semaphore()
    for dev in dev_y + dev_z + dev_t:
        pl.semaphore_signal(barrier, inc=1, device_id=dev, device_id_type=MESH)

    mine = pl.multiple_of(h * HALF, 128)
    other = pl.multiple_of((1 - h) * HALF, 128)
    own = pl.ds(mine, HALF)
    spans = [pl.ds(pl.multiple_of(base + i * STEP, 128), STEP) for base in (other, mine) for i in range(3)]
    consts = [
        pltpu.make_async_copy(src, dst, csem.at[i])
        for i, (src, dst) in enumerate(
            [(cos_hbm, cs.at[0]), (sin_hbm, cs.at[1]), (bc_hbm, bcs), (bs_hbm, bss), (small_hbm, small_ref)]
        )
    ]
    loads = [pltpu.make_async_copy(x_hbm.at[:, sp], xs.at[:, sp], xsem.at[i]) for i, sp in enumerate(spans)]
    consts[0].start()
    consts[1].start()
    for c in loads:
        c.start()
    for c in consts[2:]:
        c.start()

    live = []
    count = [0]

    def go(src, dst, where):
        i = count[0]
        count[0] += 1
        c = remote(src, dst, ssem.at[i], rsem.at[i], where)
        c.start()
        live.append(c)
        return c

    def rows(start, n):
        return pl.ds(pl.multiple_of(start, 8), n)

    idx = lax.broadcasted_iota(jnp.int32, (PATH, 1), 0)
    cv, sv = lane_turn(idx, [(t % (8 >> m)) * ROWS - ps[m] for m in range(LEVELS)])
    r = lax.broadcasted_iota(jnp.int32, (PATH, ROWS), 1)
    level = idx // RANK
    on = ((r - pick(level, ps)) & (pick(level, [16, 8, 4, 2]) - 1)) == 0
    consts[0].wait()
    consts[1].wait()
    dh, dl = split(jnp.where(on, cs[0] * cv - cs[1] * sv, 0.0))
    dboth = jnp.concatenate([dh, dl], axis=0)

    def project(i):
        loads[i].wait()
        xh, xl = split(xs[:, spans[i]])
        a = dot(dboth, xh, ((1,), (0,)))
        b = dot(dh, xl, ((1,), (0,)))
        return a[:PATH] + (a[PATH:] + b)

    first = []
    for i in range(3):
        v = project(i)
        p[:, i * STEP : (i + 1) * STEP] = v[: 3 * RANK]
        ys[96:128, spans[i]] = v[3 * RANK :]
        if i == 0:
            pl.semaphore_wait(barrier, 17)
        part = pl.ds(i * STEP, STEP)
        first.append(go(p.at[:, part], r1.at[:, part], partner))
    for i in range(3):
        v = project(3 + i)
        ys[96:128, spans[3 + i]] = v[3 * RANK :]
        part = pl.ds(i * STEP, STEP)
        first[i].wait_recv()
        sb[:, part] = v[: 3 * RANK] + r1[:, part]
    spread = []
    for d in range(1, 4):
        col = pl.ds(pl.multiple_of(lax.rem(x + d, 4) * PIECE, 128), PIECE)
        spread.append(go(sb.at[0:32, col], r3.at[d - 1], across[d - 1]))
    swap = go(sb.at[32:64, :], r2, pair_x)
    ys[64:96, own] = sb[64:96, :]
    later = [go(ys.at[64:96, own], ys.at[64:96, own], partner)]
    for c in spread:
        c.wait_recv()
    spot = pl.ds(pl.multiple_of(mine + x * PIECE, 128), PIECE)
    here = pl.ds(pl.multiple_of(x * PIECE, 128), PIECE)
    ys[0:32, spot] = (sb[0:32, here] + r3[0]) + (r3[1] + r3[2])
    place = ys.at[0:32, spot]
    back = [go(place, place, across[d - 1]) for d in range(1, 4)]
    later.append(go(place, place, partner))
    swap.wait_recv()
    ys[32:64, own] = sb[32:64, :] + r2[...]
    later.append(go(ys.at[32:64, own], ys.at[32:64, own], partner))
    for d in range(1, 4):
        back[d - 1].wait_recv()
        got = pl.ds(pl.multiple_of(mine + lax.rem(x + 4 - d, 4) * PIECE, 128), PIECE)
        later.append(go(ys.at[0:32, got], ys.at[0:32, got], partner))
    for c in later:
        c.wait_recv()
    y_copy = pltpu.make_async_copy(ys, y_hbm, csem.at[5])
    y_copy.start()

    total = None
    for i in range(6):
        part = slice(i * STEP, (i + 1) * STEP)
        xh, xl = split(xs[:, part])
        yh, yl = split(ys[:, part])
        a = dot(xh, jnp.concatenate([yh, yl], axis=0), ((1,), (1,)))
        b = dot(xl, yh, ((1,), (1,)))
        new = a[:, :PATH] + (a[:, PATH:] + b)
        if i == 0:
            acc[...] = new
        else:
            acc[...] += new
    row = 0
    for l in (2, 1, 0):
        for e in range(1 << l):
            fa[pl.ds(row, CHUNKS, stride=8), :] = acc[pl.ds(ps[l] + e * (16 >> l), CHUNKS, stride=16), :]
            row += 1
    fa[pl.ds(row, CHUNKS, stride=8), :] = jnp.zeros((CHUNKS, PATH), f32)

    def spread_y(src, dst):
        return [go(src.at[rows(y_to[d] * 64, 64)], dst.at[d], dev_y[d]) for d in range(3)]

    def spread_z(src, dst):
        return [go(src.at[rows(z_to[d] * 8, 8)], dst.at[d], dev_z[d]) for d in range(7)]

    def send_z(buf):
        piece = buf.at[rows(s * 8, 8)]
        return [go(piece, piece, dev_z[d]) for d in range(7)]

    def send_y(buf):
        band = buf.at[rows(yy * 64, 64)]
        return [go(band, band, dev_y[d]) for d in range(3)]

    def arrive(copies):
        for c in copies:
            c.wait_recv()

    def sum_y(src, got, dst):
        dst[...] = (src[rows(yy * 64, 64), :] + got[0]) + (got[1] + got[2])

    def sum_z(src, got):
        v = [src[rows(zz * 8, 8), :]] + [got[d] for d in range(7)]
        return ((v[0] + v[1]) + (v[2] + v[3])) + ((v[4] + v[5]) + (v[6] + v[7]))

    a1 = spread_y(fa, rya)
    for e in range(8):
        fb[pl.ds(e, CHUNKS, stride=8), :] = acc[pl.ds(ps[3] + 2 * e, CHUNKS, stride=16), :]
    b1 = spread_y(fb, ryb)

    for c in consts[2:]:
        c.wait()
    lane = lax.broadcasted_iota(jnp.int32, (1, PATH), 1)
    rowi = lax.broadcasted_iota(jnp.int32, (NSUB, 1), 0)
    qpad = small_ref[0]
    for l in range(1, LEVELS):
        start = (t // (8 >> l)) * (ROWS * (8 >> l)) + ps[l]
        cv, sv = lane_turn(lane, [start - (t // (8 >> m)) * (ROWS * (8 >> m)) - ps[m] for m in range(LEVELS)])
        table = bcs[l - 1] * cv - bss[l - 1] * sv
        tab[l - 1] = table
        fold[l - 1] = dot32(qpad, table, 0, 0)[:RANK]

    arrive(a1)
    sum_y(fa, rya, qa)
    a2 = spread_z(qa, rza)
    arrive(b1)
    sum_y(fb, ryb, qb)
    b2 = spread_z(qb, rzb)
    arrive(a2)
    xb[t] = sum_z(qa, rza)
    a3 = [go(xb.at[t], xb.at[t], dev_t[d]) for d in range(7)]
    arrive(b2)
    gt[rows(s * 8, 8), :] = sum_z(qb, rzb)
    arrive(a3)
    two = t // 2 * 2
    quad = t // 4 * 4
    for i in range(4):
        cb[2 * i : 2 * i + 2, :] = xb[quad + i][4:6]
    for i in range(8):
        cb[8 + i : 9 + i, :] = xb[i][6:7]
    lane8 = lax.broadcasted_iota(jnp.int32, (8, PATH), 1)
    gc[rows(s * 8, 8), :] = jnp.where(lane8 < 64, cb[0:8, :], pltpu.roll(cb[8:16, :], 64, 1))
    c4 = send_z(gc)
    gb[rows(s * 8, 8), :] = jnp.concatenate([xb[two][0:4], xb[two + 1][0:4]], axis=0)
    b4 = send_z(gb)
    t4 = send_z(gt)
    arrive(c4)
    c5 = send_y(gc)
    arrive(b4)
    b5 = send_y(gb)
    arrive(t4)
    t5 = send_y(gt)

    sub = lax.broadcasted_iota(jnp.int32, (RANK, PATH), 0)
    lan = lax.broadcasted_iota(jnp.int32, (RANK, PATH), 1)
    eye = (sub == lan).astype(f32)
    eye_next = (sub + RANK == lan).astype(f32)
    rblk = lax.broadcasted_iota(jnp.int32, (PATH, PATH), 0) // RANK
    cblk = lax.broadcasted_iota(jnp.int32, (PATH, PATH), 1) // RANK
    wq = small_ref[1]
    head_q = small_ref[2]
    gram = []

    def take_in(l):
        part = jnp.where(lane < RANK * (l + 1), lv[l], 0.0)
        gram.append(dot32(qpad, part, 0, 0)[:RANK])
        return part

    def whole_gram():
        rest = PATH - RANK * len(gram)
        low = jnp.concatenate(gram + ([jnp.zeros((rest, PATH), f32)] if rest else []), axis=0)
        return jnp.where(cblk <= rblk, low, low.T)

    def level_fit(l, part, n, full):
        comb = (sub + RANK * l == lan).astype(f32)
        if l:
            nk = dot32(n, full, 1, 0)
            comb = comb - dot32(fold[l - 1], n, 1, 0)
            part = part - dot32(tab[l - 1], nk, 1, 0)
        wide = jnp.concatenate([comb, jnp.zeros((PATH - RANK, PATH), f32)], axis=0)
        rt = dot32(part, wide, 1, 1)
        right = (
            jnp.where(rowi < NSUB - 1, rt, 0.0)
            + pltpu.roll(jnp.where(rowi > 0, pltpu.roll(rt, RANK, 1), 0.0), NSUB - 1, 0)
            + wq
        )
        narrow = rt[:, :RANK]
        w = dot32(narrow, right, 0, 0)
        head = dot32(narrow, head_q, 0, 0)
        wt = dot32(qpad[:, :RANK], rt, 0, 0)
        ridge_one = 0.1 / RANK * jnp.sum(w * eye)
        mode = jnp.where(lan < RANK, 0.5 * (pltpu.roll(w, RANK, 1) + wt), 0.0)
        ridge_two = 0.1 / RANK * jnp.sum(mode * eye)
        a, b = eliminate(w + ridge_one * eye, mode + ridge_two * eye + eye_next)
        smooth = head + dot32(w, a, 0, 0)[RANK : 2 * RANK]
        coef = dot32(b, smooth, 0, 0)[RANK : 2 * RANK]
        new = dot32(coef, comb, 0, 0)[64:96]
        n_ref[RANK * l : RANK * (l + 1), :] = new
        if l == LEVELS - 1:
            return None
        before = [n[: RANK * l]] if l else []
        return jnp.concatenate(before + [new, jnp.zeros((PATH - RANK * (l + 1), PATH), f32)], axis=0)

    arrive(c5)
    for i in range(8):
        lv[0, 32 * i : 32 * i + 32, :] = pltpu.roll(gc[pl.ds(i, CHUNKS, stride=8), :], 64, 1)
    for i in range(4):
        for e in range(2):
            lv[1, pl.ds(64 * i + e, CHUNKS, stride=2), :] = gc[pl.ds(2 * i + e, CHUNKS, stride=8), :]
    part0 = take_in(0)
    part1 = take_in(1)
    n = level_fit(0, part0, None, None)
    full = whole_gram()
    arrive(b5)
    for i in range(2):
        for e in range(4):
            lv[2, pl.ds(128 * i + e, CHUNKS, stride=4), :] = gb[pl.ds(4 * i + e, CHUNKS, stride=8), :]
    n = level_fit(1, part1, n, full)
    part2 = take_in(2)
    full = whole_gram()
    arrive(t5)
    lv[3] = gt[...]
    n = level_fit(2, part2, n, full)
    part3 = take_in(3)
    level_fit(3, part3, n, whole_gram())
    y_copy.wait()
    for c in live:
        c.wait_send()


N_COPIES = 17 + 2 * 3 + 2 * 7 + 7 + 3 * 7 + 3 * 3


def fit(phase, x, cos_t, sin_t, bc, bs, small):
    hbm = pl.BlockSpec(memory_space=pl.ANY)
    vm = pl.BlockSpec(memory_space=pltpu.VMEM)
    return pl.pallas_call(
        fit_kernel,
        in_specs=[pl.BlockSpec(memory_space=pltpu.SMEM)] + [hbm] * 6,
        out_specs=(vm, hbm),
        out_shape=(
            jax.ShapeDtypeStruct((PATH, PATH), f32),
            jax.ShapeDtypeStruct((PATH, COLS), f32),
        ),
        scratch_shapes=[
            pltpu.VMEM((ROWS, COLS), f32),
            pltpu.VMEM((PATH, COLS), f32),
            pltpu.VMEM((3 * RANK, HALF), f32),
            pltpu.VMEM((3 * RANK, HALF), f32),
            pltpu.VMEM((3 * RANK, HALF), f32),
            pltpu.VMEM((RANK, HALF), f32),
            pltpu.VMEM((3, RANK, PIECE), f32),
            pltpu.VMEM((2, PATH, ROWS), f32),
            pltpu.VMEM((3, NSUB, PATH), f32),
            pltpu.VMEM((3, NSUB, PATH), f32),
            pltpu.VMEM((3, NSUB, PATH), f32),
            pltpu.VMEM((ROWS, PATH), f32),
            pltpu.VMEM((NSUB, PATH), f32),
            pltpu.VMEM((NSUB, PATH), f32),
            pltpu.VMEM((3, 64, PATH), f32),
            pltpu.VMEM((3, 64, PATH), f32),
            pltpu.VMEM((64, PATH), f32),
            pltpu.VMEM((64, PATH), f32),
            pltpu.VMEM((7, 8, PATH), f32),
            pltpu.VMEM((7, 8, PATH), f32),
            pltpu.VMEM((8, 8, PATH), f32),
            pltpu.VMEM((16, PATH), f32),
            pltpu.VMEM((NSUB, PATH), f32),
            pltpu.VMEM((NSUB, PATH), f32),
            pltpu.VMEM((NSUB, PATH), f32),
            pltpu.VMEM((LEVELS, NSUB, PATH), f32),
            pltpu.VMEM((3, NSUB, PATH), f32),
            pltpu.VMEM((3, RANK, PATH), f32),
            pltpu.SemaphoreType.DMA((6,)),
            pltpu.SemaphoreType.DMA((6,)),
            pltpu.SemaphoreType.DMA((N_COPIES,)),
            pltpu.SemaphoreType.DMA((N_COPIES,)),
        ],
        compiler_params=pltpu.CompilerParams(
            collective_id=0, has_side_effects=True, vmem_limit_bytes=VLIM
        ),
        name="fit",
    )(phase, x, cos_t, sin_t, bc, bs, small)


def subtract_kernel(phase_ref, cos_hbm, sin_hbm, n_hbm, x_hbm, y_hbm, o_hbm, cs, ns, xs, ys, csem, xsem, ysem, osem):
    consts = [
        pltpu.make_async_copy(src, dst, csem.at[i])
        for i, (src, dst) in enumerate([(cos_hbm, cs.at[0]), (sin_hbm, cs.at[1]), (n_hbm, ns)])
    ]
    parts = [pl.ds(i * STEP, STEP) for i in range(6)]
    xl = [pltpu.make_async_copy(x_hbm.at[:, sp], xs.at[:, sp], xsem.at[i]) for i, sp in enumerate(parts)]
    yl = [pltpu.make_async_copy(y_hbm.at[:, sp], ys.at[:, sp], ysem.at[i]) for i, sp in enumerate(parts)]
    ol = [pltpu.make_async_copy(xs.at[:, sp], o_hbm.at[:, sp], osem.at[i]) for i, sp in enumerate(parts)]
    for c in consts:
        c.start()
    for a, b in zip(yl, xl):
        a.start()
        b.start()
    t = lax.axis_index("tm")
    ps = path_phases(phase_ref, t)
    idx = lax.broadcasted_iota(jnp.int32, (PATH, 1), 0)
    c, s = lane_turn(idx, [(t % (8 >> m)) * ROWS - ps[m] for m in range(LEVELS)])
    for v in consts:
        v.wait()
    eh, el = split(dot32(cs[0] * c - cs[1] * s, ns[...], 0, 0))
    e = jnp.concatenate([eh, el], axis=1)
    for i, sp in enumerate(parts):
        yl[i].wait()
        yh, ylo = split(ys[:, sp])
        fit_part = dot(e, jnp.concatenate([yh, yh], axis=0), ((1,), (0,)))
        fit_part = fit_part + dot(eh, ylo, ((1,), (0,)))
        xl[i].wait()
        xs[:, sp] = xs[:, sp] - fit_part
        ol[i].start()
    for c in ol:
        c.wait()


def subtract(phase, cos_t, sin_t, n, x, y):
    hbm = pl.BlockSpec(memory_space=pl.ANY)
    return pl.pallas_call(
        subtract_kernel,
        in_specs=[pl.BlockSpec(memory_space=pltpu.SMEM)] + [hbm] * 5,
        out_specs=hbm,
        out_shape=jax.ShapeDtypeStruct((ROWS, COLS), f32),
        scratch_shapes=[
            pltpu.VMEM((2, PATH, ROWS), f32),
            pltpu.VMEM((PATH, PATH), f32),
            pltpu.VMEM((ROWS, COLS), f32),
            pltpu.VMEM((PATH, COLS), f32),
            pltpu.SemaphoreType.DMA((3,)),
            pltpu.SemaphoreType.DMA((6,)),
            pltpu.SemaphoreType.DMA((6,)),
            pltpu.SemaphoreType.DMA((6,)),
        ],
        compiler_params=pltpu.CompilerParams(vmem_limit_bytes=VLIM),
        name="subtract",
    )(phase, cos_t, sin_t, n, x, y)


def body(snapshots, sample_phase):
    cos_t, sin_t, bc, bs, small = [jnp.asarray(v) for v in make_constants()]
    n, y = fit(sample_phase, snapshots, cos_t, sin_t, bc, bs, small)
    return subtract(sample_phase, cos_t, sin_t, n, snapshots, y)


def solution(mesh):
    return jax.shard_map(
        body,
        mesh=mesh,
        in_specs=(P("tm", "space"), P()),
        out_specs=P("tm", "space"),
        check_vma=False,
    )
```

time: 1240 us -> 71.7 us (0.06)
  waiting for transfers between devices: 932 us -> 0 us
  matrix products: 112 us -> 0 us
  blocking collectives: 78.7 us -> 0 us
  Pallas kernels: 0 us -> 70.9 us
  other arithmetic: 58.9 us -> 0 us
  local copies, waits for them, and re-layouts: 30.2 us -> 0 us
  between operations: 19.6 us -> 0.17 us
    psum x6 -> x0, waiting for transfers between devices: 932 us -> none  [the longest x3 742 us: body(): totals = lax.psum(window_buffer, ('space', 'tm'))]
    dot_general x40 -> x0, matrix products: 109 us -> none  [the longest x4 34.3 us: body(): fitted = jnp.einsum('jkc,jkp->jcp', amplitude, coords, precision=precise)]
    psum x1 -> x0, blocking collectives: 78.7 us -> none  [body(): totals = lax.psum(window_buffer, ('space', 'tm'))]
    pallas_call x0 -> x2, Pallas kernels: none -> 70.9 us  [the longest x1 61 us: fit(): pl.pallas_call(fit_kernel, in_specs=[pl.BlockSpec(memory_space=pltpu.SMEM...]
    another operation x40 -> x0, other arithmetic: 53.6 us -> none  [the longest x12 14.6 us: amplitudes(): factor_two = jnp.linalg.cholesky(mode_gram + ridge_two * identity)]
    another operation x2 -> x0, local copies, waits for them, and re-layouts: 15.7 us -> none
  transfers between devices with their start and end apart: 6 -> 0, of which waited for: 6 -> 0; matrix products, arithmetic and copies ran while one was open for 0% -> 0% of each run, Pallas kernels for 0% -> 0%
where the time goes in v2:
time: 71.7 us; the launch traced here: 71.1 us
  Pallas kernels  70.9 us (99%)
    pallas_call x1, Pallas kernels, fit(): pl.pallas_call(fit_kernel, in_specs=[pl.BlockSpec(memory_space=pltpu.SMEM...  61 us
    pallas_call x1, Pallas kernels, subtract(): pl.pallas_call(subtract_kernel, in_specs=[pl.BlockSpec(memory_space=pltpu...  9.89 us

profile of v2, /device:TPU:1, one launch (start us, length us, event | category | flops | bytes accessed | tf_op | source)
XLA Modules:
  0.0 71.1 jit_solution(5036312381230741308)
XLA Ops:
  0.0 61.0 %fit.1 = (f32[128,128]{1,0:T(8,128)}, f32[128,3072]{1,0:T(8,128)}) custom-call(s32[4,8]{1,0:T(4,128)} %phase_ref.3, f32[512,3072]{1,0:T(8,128)} %x_hbm.3, f32[128,512]{1,0:T(8,128)} %constant.10.clone.cos_hbm, f32[128,512]{1,0:T(8,128)} %constant.11.clone.sin_hbm, f32[3,256,128]{2,1,0:T(8,128)} %constant.12.clone.bc_hbm, ...), custom_call_target="tpu_custom_call" | custom-call | tf_op jit(solution)/shard_map/fit/pallas_call | solution.py:424
  61.0 9.9 %subtract.1 = f32[512,3072]{1,0:T(8,128)} custom-call(s32[4,8]{1,0:T(4,128)} %phase_ref.3, f32[128,512]{1,0:T(8,128)} %constant.10.clone.cos_hbm, f32[128,512]{1,0:T(8,128)} %constant.11.clone.sin_hbm, f32[128,128]{1,0:T(8,128)} %get-tuple-element.7.n_hbm, f32[512,3072]{1,0:T(8,128)} %x_hbm.3, f32[128,3072]{1,0:T(8,128)} %get-tuple-element.8.y_hbm), custom_call_target="tpu_custom_call" | custom-call | tf_op jit(solution)/shard_map/subtract/pallas_call | solution.py:509

commit v3 on v2

--- a/solution.py
+++ b/solution.py
@@ -16,13 +16,13 @@
 ROWS = 512
 COLS = 3072
 HALF = COLS // 2
-PIECE = HALF // 4
 CHUNKS = 32
 STEP = 512
 MESH = pl.DeviceIdType.MESH
 f32 = jnp.float32
 bf16 = jnp.bfloat16
-VLIM = 60 * 1024 * 1024
+FIT_VMEM = 20 * 1024 * 1024
+SUB_VMEM = 10 * 1024 * 1024
 
 
 def make_constants():
@@ -133,23 +133,23 @@
 
 
 def fit_kernel(
-    phase_ref, x_hbm, cos_hbm, sin_hbm, bc_hbm, bs_hbm, small_hbm, n_ref, y_hbm,
-    xs, ys, p, r1, sb, r2, r3, cs, bcs, bss, small_ref, acc, fa, fb,
-    rya, ryb, qa, qb, rza, rzb, xb, cb, gc, gb, gt, lv, tab, fold, xsem, csem, ssem, rsem,
+    phase_ref, x_hbm, cos_hbm, sin_hbm, bc_hbm, bs_hbm, small_hbm, e_ref, ys, xs,
+    p, r1, sb, rn, r2, r3, mb, cs, bcs, bss, small_ref, acc, fa, fb,
+    rya, ryb, qa, qb, rza, rzb, xb, cb, gc, gb, gt, lv, tab, tt, xsem, csem, ssem, rsem,
 ):
     s = lax.axis_index("space")
     t = lax.axis_index("tm")
-    yy, zz = s // 8, s % 8
     x, h = t // 2, t % 2
     ps = path_phases(phase_ref, t)
+    yy, zz = s // 8, s % 8
     y_to = [lax.rem(yy + d, 4) for d in range(1, 4)]
     z_to = [lax.rem(zz + d, 8) for d in range(1, 8)]
     dev_y = [{"space": v * 8 + zz} for v in y_to]
     dev_z = [{"space": yy * 8 + v} for v in z_to]
     dev_t = [{"tm": lax.rem(t + d, 8)} for d in range(1, 8)]
     partner = {"tm": x * 2 + 1 - h}
-    across = [{"tm": lax.rem(x + d, 4) * 2 + h} for d in range(1, 4)]
-    pair_x = {"tm": (x + 1 - 2 * (x % 2)) * 2 + h}
+    beside = {"tm": (x + 1 - 2 * (x % 2)) * 2 + h}
+    near = {"tm": (3 - x) * 2 + h}
 
     barrier = pltpu.get_barrier_semaphore()
     for dev in dev_y + dev_z + dev_t:
@@ -157,15 +157,17 @@
 
     mine = pl.multiple_of(h * HALF, 128)
     other = pl.multiple_of((1 - h) * HALF, 128)
-    own = pl.ds(mine, HALF)
-    spans = [pl.ds(pl.multiple_of(base + i * STEP, 128), STEP) for base in (other, mine) for i in range(3)]
+    own = [pl.ds(pl.multiple_of(mine + i * STEP, 128), STEP) for i in range(3)]
+    far = [pl.ds(pl.multiple_of(other + i * STEP, 128), STEP) for i in range(3)]
+    part = [pl.ds(i * STEP, STEP) for i in range(3)]
+    order = [far[0], far[1], own[0], far[2], own[1], own[2]]
     consts = [
         pltpu.make_async_copy(src, dst, csem.at[i])
         for i, (src, dst) in enumerate(
             [(cos_hbm, cs.at[0]), (sin_hbm, cs.at[1]), (bc_hbm, bcs), (bs_hbm, bss), (small_hbm, small_ref)]
         )
     ]
-    loads = [pltpu.make_async_copy(x_hbm.at[:, sp], xs.at[:, sp], xsem.at[i]) for i, sp in enumerate(spans)]
+    loads = [pltpu.make_async_copy(x_hbm.at[:, sp], xs.at[:, sp], xsem.at[i]) for i, sp in enumerate(order)]
     consts[0].start()
     consts[1].start()
     for c in loads:
@@ -199,65 +201,77 @@
 
     def project(i):
         loads[i].wait()
-        xh, xl = split(xs[:, spans[i]])
+        xh, xl = split(xs[:, order[i]])
         a = dot(dboth, xh, ((1,), (0,)))
         b = dot(dh, xl, ((1,), (0,)))
         return a[:PATH] + (a[PATH:] + b)
 
-    first = []
-    for i in range(3):
+    first, cross, swap, later, merge, back = [], [], [], [], [], []
+
+    def send_out(c, i):
         v = project(i)
-        p[:, i * STEP : (i + 1) * STEP] = v[: 3 * RANK]
-        ys[96:128, spans[i]] = v[3 * RANK :]
-        if i == 0:
+        p[:, part[c]] = v[: 3 * RANK]
+        ys[96:128, far[c]] = v[3 * RANK :]
+        if c == 0:
             pl.semaphore_wait(barrier, 17)
-        part = pl.ds(i * STEP, STEP)
-        first.append(go(p.at[:, part], r1.at[:, part], partner))
-    for i in range(3):
-        v = project(3 + i)
-        ys[96:128, spans[3 + i]] = v[3 * RANK :]
-        part = pl.ds(i * STEP, STEP)
-        first[i].wait_recv()
-        sb[:, part] = v[: 3 * RANK] + r1[:, part]
-    spread = []
-    for d in range(1, 4):
-        col = pl.ds(pl.multiple_of(lax.rem(x + d, 4) * PIECE, 128), PIECE)
-        spread.append(go(sb.at[0:32, col], r3.at[d - 1], across[d - 1]))
-    swap = go(sb.at[32:64, :], r2, pair_x)
-    ys[64:96, own] = sb[64:96, :]
-    later = [go(ys.at[64:96, own], ys.at[64:96, own], partner)]
-    for c in spread:
-        c.wait_recv()
-    spot = pl.ds(pl.multiple_of(mine + x * PIECE, 128), PIECE)
-    here = pl.ds(pl.multiple_of(x * PIECE, 128), PIECE)
-    ys[0:32, spot] = (sb[0:32, here] + r3[0]) + (r3[1] + r3[2])
-    place = ys.at[0:32, spot]
-    back = [go(place, place, across[d - 1]) for d in range(1, 4)]
-    later.append(go(place, place, partner))
-    swap.wait_recv()
-    ys[32:64, own] = sb[32:64, :] + r2[...]
-    later.append(go(ys.at[32:64, own], ys.at[32:64, own], partner))
-    for d in range(1, 4):
-        back[d - 1].wait_recv()
-        got = pl.ds(pl.multiple_of(mine + lax.rem(x + 4 - d, 4) * PIECE, 128), PIECE)
-        later.append(go(ys.at[0:32, got], ys.at[0:32, got], partner))
-    for c in later:
-        c.wait_recv()
-    y_copy = pltpu.make_async_copy(ys, y_hbm, csem.at[5])
-    y_copy.start()
-
-    total = None
-    for i in range(6):
-        part = slice(i * STEP, (i + 1) * STEP)
-        xh, xl = split(xs[:, part])
-        yh, yl = split(ys[:, part])
+        first.append(go(p.at[:, part[c]], r1.at[:, part[c]], partner))
+
+    def keep(c, i):
+        v = project(i)
+        sb[:, part[c]] = v[: 3 * RANK]
+        ys[96:128, own[c]] = v[3 * RANK :]
+
+    block = x // 2
+    mine_blk = [pl.ds(pl.multiple_of(c * STEP + block * 256, 128), 256) for c in range(3)]
+    away_blk = [pl.ds(pl.multiple_of(c * STEP + (1 - block) * 256, 128), 256) for c in range(3)]
+    place_blk = [pl.ds(pl.multiple_of(mine + c * STEP + block * 256, 128), 256) for c in range(3)]
+
+    def step_one(c):
+        first[c].wait_recv()
+        sb[:, part[c]] = sb[:, part[c]] + r1[:, part[c]]
+        cross.append(go(sb.at[0:32, away_blk[c]], rn.at[c], near))
+        swap.append(go(sb.at[32:64, part[c]], r2.at[c], beside))
+        ys[64:96, own[c]] = sb[64:96, part[c]]
+        later.append([go(ys.at[64:96, own[c]], ys.at[64:96, own[c]], partner)])
+
+    send_out(0, 0)
+    send_out(1, 1)
+    keep(0, 2)
+    step_one(0)
+    send_out(2, 3)
+    keep(1, 4)
+    step_one(1)
+    keep(2, 5)
+    step_one(2)
+    for c in range(3):
+        cross[c].wait_recv()
+        mb[c] = sb[0:32, mine_blk[c]] + rn[c]
+        merge.append(go(mb.at[c], r3.at[c], beside))
+    for c in range(3):
+        swap[c].wait_recv()
+        ys[32:64, own[c]] = sb[32:64, part[c]] + r2[c]
+        later[c].append(go(ys.at[32:64, own[c]], ys.at[32:64, own[c]], partner))
+        merge[c].wait_recv()
+        ys[0:32, place_blk[c]] = mb[c] + r3[c]
+        back.append(go(ys.at[0:32, place_blk[c]], ys.at[0:32, place_blk[c]], near))
+    for c in range(3):
+        back[c].wait_recv()
+        later[c].append(go(ys.at[0:32, own[c]], ys.at[0:32, own[c]], partner))
+
+    def product(sp):
+        xh, xl = split(xs[:, sp])
+        yh, yl = split(ys[:, sp])
         a = dot(xh, jnp.concatenate([yh, yl], axis=0), ((1,), (1,)))
         b = dot(xl, yh, ((1,), (1,)))
-        new = a[:, :PATH] + (a[:, PATH:] + b)
-        if i == 0:
-            acc[...] = new
-        else:
-            acc[...] += new
+        return a[:, :PATH] + (a[:, PATH:] + b)
+
+    acc[...] = product(own[0])
+    acc[...] += product(own[1])
+    acc[...] += product(own[2])
+    for c in range(3):
+        for v in later[c]:
+            v.wait_recv()
+        acc[...] += product(far[c])
     row = 0
     for l in (2, 1, 0):
         for e in range(1 << l):
@@ -302,10 +316,11 @@
     qpad = small_ref[0]
     for l in range(1, LEVELS):
         start = (t // (8 >> l)) * (ROWS * (8 >> l)) + ps[l]
-        cv, sv = lane_turn(lane, [start - (t // (8 >> m)) * (ROWS * (8 >> m)) - ps[m] for m in range(LEVELS)])
-        table = bcs[l - 1] * cv - bss[l - 1] * sv
-        tab[l - 1] = table
-        fold[l - 1] = dot32(qpad, table, 0, 0)[:RANK]
+        ca, sa = lane_turn(lane, [start - (t // (8 >> m)) * (ROWS * (8 >> m)) - ps[m] for m in range(LEVELS)])
+        table = bcs[l - 1] * ca - bss[l - 1] * sa
+        tab[l - 1, 0:NSUB, :] = table
+        tab[l - 1, NSUB:, :] = dot32(qpad, table, 0, 0)[:RANK]
+    tt[...] = (cs[0] * cv - cs[1] * sv).T
 
     arrive(a1)
     sum_y(fa, rya, qa)
@@ -346,26 +361,23 @@
     cblk = lax.broadcasted_iota(jnp.int32, (PATH, PATH), 1) // RANK
     wq = small_ref[1]
     head_q = small_ref[2]
-    gram = []
+    gram, seen, fits = [], [], []
 
     def take_in(l):
-        part = jnp.where(lane < RANK * (l + 1), lv[l], 0.0)
-        gram.append(dot32(qpad, part, 0, 0)[:RANK])
-        return part
+        v = jnp.where(lane < RANK * (l + 1), lv[l], 0.0)
+        seen.append(v)
+        gram.append(dot32(qpad, v, 0, 0)[:RANK])
+
+    def fill(blocks):
+        rest = PATH - RANK * len(blocks)
+        return jnp.concatenate(blocks + ([jnp.zeros((rest, PATH), f32)] if rest else []), axis=0)
 
     def whole_gram():
-        rest = PATH - RANK * len(gram)
-        low = jnp.concatenate(gram + ([jnp.zeros((rest, PATH), f32)] if rest else []), axis=0)
+        low = fill(gram)
         return jnp.where(cblk <= rblk, low, low.T)
 
-    def level_fit(l, part, n, full):
-        comb = (sub + RANK * l == lan).astype(f32)
-        if l:
-            nk = dot32(n, full, 1, 0)
-            comb = comb - dot32(fold[l - 1], n, 1, 0)
-            part = part - dot32(tab[l - 1], nk, 1, 0)
-        wide = jnp.concatenate([comb, jnp.zeros((PATH - RANK, PATH), f32)], axis=0)
-        rt = dot32(part, wide, 1, 1)
+    def level_fit(l, part, comb):
+        rt = dot32(part, fill([comb]), 1, 1)
         right = (
             jnp.where(rowi < NSUB - 1, rt, 0.0)
             + pltpu.roll(jnp.where(rowi > 0, pltpu.roll(rt, RANK, 1), 0.0), NSUB - 1, 0)
@@ -380,13 +392,24 @@
         ridge_two = 0.1 / RANK * jnp.sum(mode * eye)
         a, b = eliminate(w + ridge_one * eye, mode + ridge_two * eye + eye_next)
         smooth = head + dot32(w, a, 0, 0)[RANK : 2 * RANK]
-        coef = dot32(b, smooth, 0, 0)[RANK : 2 * RANK]
-        new = dot32(coef, comb, 0, 0)[64:96]
-        n_ref[RANK * l : RANK * (l + 1), :] = new
-        if l == LEVELS - 1:
-            return None
-        before = [n[: RANK * l]] if l else []
-        return jnp.concatenate(before + [new, jnp.zeros((PATH - RANK * (l + 1), PATH), f32)], axis=0)
+        mc = dot32(b, comb, 0, 0)[RANK : 2 * RANK]
+        moved = jnp.where((lan >= 64) & (lan < 96), smooth, 0.0)
+        if l != 2:
+            moved = pltpu.roll(moved, (RANK * l - 64) % PATH, 1)
+        fits.append(dot32(moved, mc, 0, 0)[RANK * l : RANK * (l + 1)])
+        return moved, mc
+
+    def advance(l, moved, mc):
+        full = whole_gram()
+        both = tab[l - 1]
+        lead = dot32(both, moved, 1, 1)
+        comb = (sub + RANK * l == lan).astype(f32) - dot32(lead[NSUB:], mc, 1, 0)
+        part = seen[l] - dot32(lead[:NSUB], dot32(mc, full, 1, 0), 1, 0)
+        if l > 1:
+            n = fill(fits[: l - 1])
+            comb = comb - dot32(both[NSUB:], n, 1, 0)
+            part = part - dot32(both[:NSUB], dot32(n, full, 1, 0), 1, 0)
+        return part, comb
 
     arrive(c5)
     for i in range(8):
@@ -394,49 +417,53 @@
     for i in range(4):
         for e in range(2):
             lv[1, pl.ds(64 * i + e, CHUNKS, stride=2), :] = gc[pl.ds(2 * i + e, CHUNKS, stride=8), :]
-    part0 = take_in(0)
-    part1 = take_in(1)
-    n = level_fit(0, part0, None, None)
-    full = whole_gram()
+    take_in(0)
+    take_in(1)
+    moved, mc = level_fit(0, seen[0], eye)
+    nxt = advance(1, moved, mc)
     arrive(b5)
     for i in range(2):
         for e in range(4):
             lv[2, pl.ds(128 * i + e, CHUNKS, stride=4), :] = gb[pl.ds(4 * i + e, CHUNKS, stride=8), :]
-    n = level_fit(1, part1, n, full)
-    part2 = take_in(2)
-    full = whole_gram()
+    take_in(2)
+    moved, mc = level_fit(1, *nxt)
+    nxt = advance(2, moved, mc)
+    moved, mc = level_fit(2, *nxt)
     arrive(t5)
     lv[3] = gt[...]
-    n = level_fit(2, part2, n, full)
-    part3 = take_in(3)
-    level_fit(3, part3, n, whole_gram())
-    y_copy.wait()
+    take_in(3)
+    nxt = advance(3, moved, mc)
+    level_fit(3, *nxt)
+    eh, el = split(dot32(tt[...], fill(fits), 1, 0))
+    e_ref[:, :PATH] = eh
+    e_ref[:, PATH:] = el
     for c in live:
         c.wait_send()
 
 
-N_COPIES = 17 + 2 * 3 + 2 * 7 + 7 + 3 * 7 + 3 * 3
+N_COPIES = 24 + 5 * 7 + 5 * 3 + 7
 
 
 def fit(phase, x, cos_t, sin_t, bc, bs, small):
-    hbm = pl.BlockSpec(memory_space=pl.ANY)
+    hbm = pl.BlockSpec(memory_space=pltpu.HBM)
     vm = pl.BlockSpec(memory_space=pltpu.VMEM)
     return pl.pallas_call(
         fit_kernel,
         in_specs=[pl.BlockSpec(memory_space=pltpu.SMEM)] + [hbm] * 6,
-        out_specs=(vm, hbm),
+        out_specs=(vm, vm, vm),
         out_shape=(
-            jax.ShapeDtypeStruct((PATH, PATH), f32),
+            jax.ShapeDtypeStruct((ROWS, 2 * PATH), bf16),
             jax.ShapeDtypeStruct((PATH, COLS), f32),
+            jax.ShapeDtypeStruct((ROWS, COLS), f32),
         ),
         scratch_shapes=[
-            pltpu.VMEM((ROWS, COLS), f32),
-            pltpu.VMEM((PATH, COLS), f32),
             pltpu.VMEM((3 * RANK, HALF), f32),
             pltpu.VMEM((3 * RANK, HALF), f32),
             pltpu.VMEM((3 * RANK, HALF), f32),
-            pltpu.VMEM((RANK, HALF), f32),
-            pltpu.VMEM((3, RANK, PIECE), f32),
+            pltpu.VMEM((3, RANK, 256), f32),
+            pltpu.VMEM((3, RANK, STEP), f32),
+            pltpu.VMEM((3, RANK, 256), f32),
+            pltpu.VMEM((3, RANK, 256), f32),
             pltpu.VMEM((2, PATH, ROWS), f32),
             pltpu.VMEM((3, NSUB, PATH), f32),
             pltpu.VMEM((3, NSUB, PATH), f32),
@@ -456,80 +483,55 @@
             pltpu.VMEM((NSUB, PATH), f32),
             pltpu.VMEM((NSUB, PATH), f32),
             pltpu.VMEM((LEVELS, NSUB, PATH), f32),
-            pltpu.VMEM((3, NSUB, PATH), f32),
-            pltpu.VMEM((3, RANK, PATH), f32),
+            pltpu.VMEM((3, NSUB + RANK, PATH), f32),
+            pltpu.VMEM((ROWS, PATH), f32),
             pltpu.SemaphoreType.DMA((6,)),
-            pltpu.SemaphoreType.DMA((6,)),
+            pltpu.SemaphoreType.DMA((5,)),
             pltpu.SemaphoreType.DMA((N_COPIES,)),
             pltpu.SemaphoreType.DMA((N_COPIES,)),
         ],
         compiler_params=pltpu.CompilerParams(
-            collective_id=0, has_side_effects=True, vmem_limit_bytes=VLIM
+            collective_id=0, has_side_effects=True, vmem_limit_bytes=FIT_VMEM
         ),
         name="fit",
     )(phase, x, cos_t, sin_t, bc, bs, small)
 
 
-def subtract_kernel(phase_ref, cos_hbm, sin_hbm, n_hbm, x_hbm, y_hbm, o_hbm, cs, ns, xs, ys, csem, xsem, ysem, osem):
-    consts = [
-        pltpu.make_async_copy(src, dst, csem.at[i])
-        for i, (src, dst) in enumerate([(cos_hbm, cs.at[0]), (sin_hbm, cs.at[1]), (n_hbm, ns)])
-    ]
-    parts = [pl.ds(i * STEP, STEP) for i in range(6)]
-    xl = [pltpu.make_async_copy(x_hbm.at[:, sp], xs.at[:, sp], xsem.at[i]) for i, sp in enumerate(parts)]
-    yl = [pltpu.make_async_copy(y_hbm.at[:, sp], ys.at[:, sp], ysem.at[i]) for i, sp in enumerate(parts)]
-    ol = [pltpu.make_async_copy(xs.at[:, sp], o_hbm.at[:, sp], osem.at[i]) for i, sp in enumerate(parts)]
-    for c in consts:
-        c.start()
-    for a, b in zip(yl, xl):
-        a.start()
-        b.start()
-    t = lax.axis_index("tm")
-    ps = path_phases(phase_ref, t)
-    idx = lax.broadcasted_iota(jnp.int32, (PATH, 1), 0)
-    c, s = lane_turn(idx, [(t % (8 >> m)) * ROWS - ps[m] for m in range(LEVELS)])
-    for v in consts:
-        v.wait()
-    eh, el = split(dot32(cs[0] * c - cs[1] * s, ns[...], 0, 0))
-    e = jnp.concatenate([eh, el], axis=1)
-    for i, sp in enumerate(parts):
-        yl[i].wait()
-        yh, ylo = split(ys[:, sp])
-        fit_part = dot(e, jnp.concatenate([yh, yh], axis=0), ((1,), (0,)))
-        fit_part = fit_part + dot(eh, ylo, ((1,), (0,)))
-        xl[i].wait()
-        xs[:, sp] = xs[:, sp] - fit_part
-        ol[i].start()
-    for c in ol:
+def subtract_kernel(e_ref, x_ref, y_ref, o_hbm, rest, osem):
+    e = e_ref[...]
+    copies = []
+    for i in range(6):
+        sp = pl.ds(i * STEP, STEP)
+        yh, yl = split(y_ref[:, sp])
+        fitted = dot(e, jnp.concatenate([yh, yh], axis=0), ((1,), (0,)))
+        fitted = fitted + dot(e[:, :PATH], yl, ((1,), (0,)))
+        rest[:, sp] = x_ref[:, sp] - fitted
+        copies.append(pltpu.make_async_copy(rest.at[:, sp], o_hbm.at[:, sp], osem.at[i]))
+        copies[i].start()
+    for c in copies:
         c.wait()
 
 
-def subtract(phase, cos_t, sin_t, n, x, y):
-    hbm = pl.BlockSpec(memory_space=pl.ANY)
+def subtract(e, x, y):
+    vm = pl.BlockSpec(memory_space=pltpu.VMEM)
     return pl.pallas_call(
         subtract_kernel,
-        in_specs=[pl.BlockSpec(memory_space=pltpu.SMEM)] + [hbm] * 5,
-        out_specs=hbm,
+        in_specs=[vm] * 3,
+        out_specs=pl.BlockSpec(memory_space=pltpu.HBM),
         out_shape=jax.ShapeDtypeStruct((ROWS, COLS), f32),
-        scratch_shapes=[
-            pltpu.VMEM((2, PATH, ROWS), f32),
-            pltpu.VMEM((PATH, PATH), f32),
-            pltpu.VMEM((ROWS, COLS), f32),
-            pltpu.VMEM((PATH, COLS), f32),
-            pltpu.SemaphoreType.DMA((3,)),
-            pltpu.SemaphoreType.DMA((6,)),
-            pltpu.SemaphoreType.DMA((6,)),
-            pltpu.SemaphoreType.DMA((6,)),
-        ],
-        compiler_params=pltpu.CompilerParams(vmem_limit_bytes=VLIM),
+        scratch_shapes=[pltpu.VMEM((ROWS, COLS), f32), pltpu.SemaphoreType.DMA((6,))],
+        compiler_params=pltpu.CompilerParams(vmem_limit_bytes=SUB_VMEM),
         name="subtract",
-    )(phase, cos_t, sin_t, n, x, y)
+    )(e, x, y)
 
 
 def body(snapshots, sample_phase):
-    cos_t, sin_t, bc, bs, small = [jnp.asarray(v) for v in make_constants()]
-    n, y = fit(sample_phase, snapshots, cos_t, sin_t, bc, bs, small)
-    return subtract(sample_phase, cos_t, sin_t, n, snapshots, y)
+    stay = [
+        pltpu.with_memory_space_constraint(v, pltpu.HBM)
+        for v in [snapshots] + [jnp.asarray(c) for c in make_constants()]
+    ]
+    e, y, held = fit(pltpu.with_memory_space_constraint(sample_phase, pltpu.HBM), *stay)
+    return subtract(e, held, y)
 
 
 def solution(mesh):

time: 71.7 us -> 64.9 us (0.905)
  Pallas kernels: 70.9 us -> 64 us
    pallas_call x1, Pallas kernels: 9.89 us -> 3.16 us  [subtract(): pl.pallas_call(subtract_kernel, in_specs=[vm] * 3, out_specs=pl.BlockSpec...]
where the time goes in v3:
time: 64.9 us; the launch traced here: 64.2 us
  Pallas kernels  64 us (99%)
    pallas_call x1, Pallas kernels, fit(): pl.pallas_call(fit_kernel, in_specs=[pl.BlockSpec(memory_space=pltpu.SMEM...  60.8 us
    pallas_call x1, Pallas kernels, subtract(): pl.pallas_call(subtract_kernel, in_specs=[vm] * 3, out_specs=pl.BlockSpec...  3.16 us

profile of v3, /device:TPU:1, one launch (start us, length us, event | category | flops | bytes accessed | tf_op | source)
XLA Modules:
  0.0 64.2 jit_solution(7840639607196557565)
XLA Ops:
  0.0 60.8 %fit.1 = (bf16[512,256]{1,0:T(8,128)(2,1)S(1)}, f32[128,3072]{1,0:T(8,128)S(1)}, f32[512,3072]{1,0:T(8,128)S(1)}) custom-call(s32[4,8]{1,0:T(4,128)} %phase_ref.1, f32[512,3072]{1,0:T(8,128)} %x_hbm.1, f32[128,512]{1,0:T(8,128)} %constant.10.clone.cos_hbm, f32[128,512]{1,0:T(8,128)} %constant.11.clone.sin_hbm, f32[3,256,128]{2,1,0:T(8,128)} %constant.12.clone.bc_hbm, ...), custom_call_target="tpu_custom_call" | custom-call | tf_op jit(solution)/shard_map/fit/pallas_call | solution.py:450
  60.8 3.2 %subtract.1 = f32[512,3072]{1,0:T(8,128)} custom-call(bf16[512,256]{1,0:T(8,128)(2,1)S(1)} %get-tuple-element.8.e_ref, f32[512,3072]{1,0:T(8,128)S(1)} %get-tuple-element.9.x_ref, f32[128,3072]{1,0:T(8,128)S(1)} %get-tuple-element.10.y_ref), custom_call_target="tpu_custom_call" | custom-call | tf_op jit(solution)/shard_map/subtract/pallas_call | solution.py:517

commit v4 on v3

--- a/solution.py
+++ b/solution.py
@@ -103,6 +103,13 @@
     )
 
 
+def dot3(a, b, ca, cb):
+    ah, al = split(a)
+    bh, bl = split(b)
+    dims = ((ca,), (cb,))
+    return dot(ah, bh, dims) + (dot(ah, bl, dims) + dot(al, bh, dims))
+
+
 def remote(src, dst, send, recv, where):
     return pltpu.make_async_remote_copy(
         src_ref=src, dst_ref=dst, send_sem=send, recv_sem=recv, device_id=where, device_id_type=MESH
@@ -226,11 +233,15 @@
     away_blk = [pl.ds(pl.multiple_of(c * STEP + (1 - block) * 256, 128), 256) for c in range(3)]
     place_blk = [pl.ds(pl.multiple_of(mine + c * STEP + block * 256, 128), 256) for c in range(3)]
 
+    def trade(c):
+        swap.append(go(sb.at[32:64, part[c]], r2.at[c], beside))
+
     def step_one(c):
         first[c].wait_recv()
         sb[:, part[c]] = sb[:, part[c]] + r1[:, part[c]]
         cross.append(go(sb.at[0:32, away_blk[c]], rn.at[c], near))
-        swap.append(go(sb.at[32:64, part[c]], r2.at[c], beside))
+        if c == 0:
+            trade(c)
         ys[64:96, own[c]] = sb[64:96, part[c]]
         later.append([go(ys.at[64:96, own[c]], ys.at[64:96, own[c]], partner)])
 
@@ -247,13 +258,16 @@
         cross[c].wait_recv()
         mb[c] = sb[0:32, mine_blk[c]] + rn[c]
         merge.append(go(mb.at[c], r3.at[c], beside))
+    trade(1)
+    trade(2)
+    for c in range(3):
+        merge[c].wait_recv()
+        ys[0:32, place_blk[c]] = mb[c] + r3[c]
+        back.append(go(ys.at[0:32, place_blk[c]], ys.at[0:32, place_blk[c]], near))
     for c in range(3):
         swap[c].wait_recv()
         ys[32:64, own[c]] = sb[32:64, part[c]] + r2[c]
         later[c].append(go(ys.at[32:64, own[c]], ys.at[32:64, own[c]], partner))
-        merge[c].wait_recv()
-        ys[0:32, place_blk[c]] = mb[c] + r3[c]
-        back.append(go(ys.at[0:32, place_blk[c]], ys.at[0:32, place_blk[c]], near))
     for c in range(3):
         back[c].wait_recv()
         later[c].append(go(ys.at[0:32, own[c]], ys.at[0:32, own[c]], partner))
@@ -376,8 +390,11 @@
         low = fill(gram)
         return jnp.where(cblk <= rblk, low, low.T)
 
+    def trace(v):
+        return jnp.sum(jnp.sum(v * eye, axis=0, keepdims=True), axis=1, keepdims=True)
+
     def level_fit(l, part, comb):
-        rt = dot32(part, fill([comb]), 1, 1)
+        rt = dot3(part, fill([comb]), 1, 1) if l else part
         right = (
             jnp.where(rowi < NSUB - 1, rt, 0.0)
             + pltpu.roll(jnp.where(rowi > 0, pltpu.roll(rt, RANK, 1), 0.0), NSUB - 1, 0)
@@ -387,9 +404,9 @@
         w = dot32(narrow, right, 0, 0)
         head = dot32(narrow, head_q, 0, 0)
         wt = dot32(qpad[:, :RANK], rt, 0, 0)
-        ridge_one = 0.1 / RANK * jnp.sum(w * eye)
+        ridge_one = 0.1 / RANK * trace(w)
         mode = jnp.where(lan < RANK, 0.5 * (pltpu.roll(w, RANK, 1) + wt), 0.0)
-        ridge_two = 0.1 / RANK * jnp.sum(mode * eye)
+        ridge_two = 0.1 / RANK * trace(mode)
         a, b = eliminate(w + ridge_one * eye, mode + ridge_two * eye + eye_next)
         smooth = head + dot32(w, a, 0, 0)[RANK : 2 * RANK]
         mc = dot32(b, comb, 0, 0)[RANK : 2 * RANK]
@@ -402,13 +419,13 @@
     def advance(l, moved, mc):
         full = whole_gram()
         both = tab[l - 1]
-        lead = dot32(both, moved, 1, 1)
-        comb = (sub + RANK * l == lan).astype(f32) - dot32(lead[NSUB:], mc, 1, 0)
-        part = seen[l] - dot32(lead[:NSUB], dot32(mc, full, 1, 0), 1, 0)
+        lead = dot3(both, moved, 1, 1)
+        comb = (sub + RANK * l == lan).astype(f32) - dot3(lead[NSUB:], mc, 1, 0)
+        part = seen[l] - dot3(lead[:NSUB], dot3(mc, full, 1, 0), 1, 0)
         if l > 1:
             n = fill(fits[: l - 1])
-            comb = comb - dot32(both[NSUB:], n, 1, 0)
-            part = part - dot32(both[:NSUB], dot32(n, full, 1, 0), 1, 0)
+            comb = comb - dot3(both[NSUB:], n, 1, 0)
+            part = part - dot3(both[:NSUB], dot3(n, full, 1, 0), 1, 0)
         return part, comb
 
     arrive(c5)

time: 64.9 us -> 62.6 us (0.965)
  Pallas kernels: 64 us -> 62 us
    pallas_call x1, Pallas kernels: 60.8 us -> 58.9 us  [fit(): pl.pallas_call(fit_kernel, in_specs=[pl.BlockSpec(memory_space=pltpu.SMEM...]
where the time goes in v4:
time: 62.6 us; the launch traced here: 62.2 us
  Pallas kernels  62 us (99%)
    pallas_call x1, Pallas kernels, fit(): pl.pallas_call(fit_kernel, in_specs=[pl.BlockSpec(memory_space=pltpu.SMEM...  58.9 us
    pallas_call x1, Pallas kernels, subtract(): pl.pallas_call(subtract_kernel, in_specs=[vm] * 3, out_specs=pl.BlockSpec...  3.15 us

profile of v4, /device:TPU:1, one launch (start us, length us, event | category | flops | bytes accessed | tf_op | source)
XLA Modules:
  0.0 62.2 jit_solution(10601187000912151970)
XLA Ops:
  0.0 58.9 %fit.1 = (bf16[512,256]{1,0:T(8,128)(2,1)S(1)}, f32[128,3072]{1,0:T(8,128)S(1)}, f32[512,3072]{1,0:T(8,128)S(1)}) custom-call(s32[4,8]{1,0:T(4,128)} %phase_ref.1, f32[512,3072]{1,0:T(8,128)} %x_hbm.1, f32[128,512]{1,0:T(8,128)} %constant.10.clone.cos_hbm, f32[128,512]{1,0:T(8,128)} %constant.11.clone.sin_hbm, f32[3,256,128]{2,1,0:T(8,128)} %constant.12.clone.bc_hbm, ...), custom_call_target="tpu_custom_call" | custom-call | tf_op jit(solution)/shard_map/fit/pallas_call | solution.py:467
  58.9 3.2 %subtract.1 = f32[512,3072]{1,0:T(8,128)} custom-call(bf16[512,256]{1,0:T(8,128)(2,1)S(1)} %get-tuple-element.8.e_ref, f32[512,3072]{1,0:T(8,128)S(1)} %get-tuple-element.9.x_ref, f32[128,3072]{1,0:T(8,128)S(1)} %get-tuple-element.10.y_ref), custom_call_target="tpu_custom_call" | custom-call | tf_op jit(solution)/shard_map/subtract/pallas_call | solution.py:534

commit v5 on v4

--- a/solution.py
+++ b/solution.py
@@ -321,7 +321,6 @@
     a1 = spread_y(fa, rya)
     for e in range(8):
         fb[pl.ds(e, CHUNKS, stride=8), :] = acc[pl.ds(ps[3] + 2 * e, CHUNKS, stride=16), :]
-    b1 = spread_y(fb, ryb)
 
     for c in consts[2:]:
         c.wait()
@@ -339,14 +338,13 @@
     arrive(a1)
     sum_y(fa, rya, qa)
     a2 = spread_z(qa, rza)
+    b1 = spread_y(fb, ryb)
+    arrive(a2)
+    xb[t] = sum_z(qa, rza)
+    a3 = [go(xb.at[t], xb.at[t], dev_t[d]) for d in range(7)]
     arrive(b1)
     sum_y(fb, ryb, qb)
     b2 = spread_z(qb, rzb)
-    arrive(a2)
-    xb[t] = sum_z(qa, rza)
-    a3 = [go(xb.at[t], xb.at[t], dev_t[d]) for d in range(7)]
-    arrive(b2)
-    gt[rows(s * 8, 8), :] = sum_z(qb, rzb)
     arrive(a3)
     two = t // 2 * 2
     quad = t // 4 * 4
@@ -359,13 +357,13 @@
     c4 = send_z(gc)
     gb[rows(s * 8, 8), :] = jnp.concatenate([xb[two][0:4], xb[two + 1][0:4]], axis=0)
     b4 = send_z(gb)
-    t4 = send_z(gt)
     arrive(c4)
     c5 = send_y(gc)
     arrive(b4)
     b5 = send_y(gb)
-    arrive(t4)
-    t5 = send_y(gt)
+    arrive(b2)
+    gt[rows(s * 8, 8), :] = sum_z(qb, rzb)
+    t4 = send_z(gt)
 
     sub = lax.broadcasted_iota(jnp.int32, (RANK, PATH), 0)
     lan = lax.broadcasted_iota(jnp.int32, (RANK, PATH), 1)
@@ -408,12 +406,12 @@
         mode = jnp.where(lan < RANK, 0.5 * (pltpu.roll(w, RANK, 1) + wt), 0.0)
         ridge_two = 0.1 / RANK * trace(mode)
         a, b = eliminate(w + ridge_one * eye, mode + ridge_two * eye + eye_next)
-        smooth = head + dot32(w, a, 0, 0)[RANK : 2 * RANK]
+        smooth = head + dot3(w, a, 0, 0)[RANK : 2 * RANK]
         mc = dot32(b, comb, 0, 0)[RANK : 2 * RANK]
         moved = jnp.where((lan >= 64) & (lan < 96), smooth, 0.0)
         if l != 2:
             moved = pltpu.roll(moved, (RANK * l - 64) % PATH, 1)
-        fits.append(dot32(moved, mc, 0, 0)[RANK * l : RANK * (l + 1)])
+        fits.append(dot3(moved, mc, 0, 0)[RANK * l : RANK * (l + 1)])
         return moved, mc
 
     def advance(l, moved, mc):
@@ -438,6 +436,8 @@
     take_in(1)
     moved, mc = level_fit(0, seen[0], eye)
     nxt = advance(1, moved, mc)
+    arrive(t4)
+    t5 = send_y(gt)
     arrive(b5)
     for i in range(2):
         for e in range(4):
@@ -451,7 +451,7 @@
     take_in(3)
     nxt = advance(3, moved, mc)
     level_fit(3, *nxt)
-    eh, el = split(dot32(tt[...], fill(fits), 1, 0))
+    eh, el = split(dot3(tt[...], fill(fits), 1, 0))
     e_ref[:, :PATH] = eh
     e_ref[:, PATH:] = el
     for c in live:

time: 62.6 us -> 61.3 us (0.979)
  Pallas kernels: 62 us -> 61.2 us
    pallas_call x1, Pallas kernels: 58.9 us -> 58.1 us  [fit(): pl.pallas_call(fit_kernel, in_specs=[pl.BlockSpec(memory_space=pltpu.SMEM...]
where the time goes in v5:
time: 61.3 us; the launch traced here: 61.2 us
  Pallas kernels  61.2 us (100%)
    pallas_call x1, Pallas kernels, fit(): pl.pallas_call(fit_kernel, in_specs=[pl.BlockSpec(memory_space=pltpu.SMEM...  58.1 us
    pallas_call x1, Pallas kernels, subtract(): pl.pallas_call(subtract_kernel, in_specs=[vm] * 3, out_specs=pl.BlockSpec...  3.16 us

profile of v5, /device:TPU:1, one launch (start us, length us, event | category | flops | bytes accessed | tf_op | source)
XLA Modules:
  0.0 61.2 jit_solution(10265786095073682258)
XLA Ops:
  0.0 58.1 %fit.1 = (bf16[512,256]{1,0:T(8,128)(2,1)S(1)}, f32[128,3072]{1,0:T(8,128)S(1)}, f32[512,3072]{1,0:T(8,128)S(1)}) custom-call(s32[4,8]{1,0:T(4,128)} %phase_ref.1, f32[512,3072]{1,0:T(8,128)} %x_hbm.1, f32[128,512]{1,0:T(8,128)} %constant.10.clone.cos_hbm, f32[128,512]{1,0:T(8,128)} %constant.11.clone.sin_hbm, f32[3,256,128]{2,1,0:T(8,128)} %constant.12.clone.bc_hbm, ...), custom_call_target="tpu_custom_call" | custom-call | tf_op jit(solution)/shard_map/fit/pallas_call | solution.py:467
  58.1 3.2 %subtract.1 = f32[512,3072]{1,0:T(8,128)} custom-call(bf16[512,256]{1,0:T(8,128)(2,1)S(1)} %get-tuple-element.8.e_ref, f32[512,3072]{1,0:T(8,128)S(1)} %get-tuple-element.9.x_ref, f32[128,3072]{1,0:T(8,128)S(1)} %get-tuple-element.10.y_ref), custom_call_target="tpu_custom_call" | custom-call | tf_op jit(solution)/shard_map/subtract/pallas_call | solution.py:534
